TPU v7x, 32 devices: a whole 2x2x4 slice. The times are simulated.
32 devices in a mesh: seg: 4 (over y, x), blk: 8 (over z, core).
Axes of the slice: x: 2, y: 2, z: 4, core: 2. Of those that a mesh axis runs over, the one named last changes fastest.
Arguments:
- psi_init: float32 [4, 128, 128, 128], P('seg', 'blk'), may hold values from -6 to 6
- env_left: bfloat16 [4, 48, 8, 128, 128], P('seg', 'blk'), may hold values from -0.5 to 0.5
- env_right: bfloat16 [4, 48, 8, 128, 128], P('seg', 'blk'), may hold values from -0.5 to 0.5
- coef: float32 [4, 48, 128], P('seg', 'blk'), may hold values from -1.25 to 1.25
- source: int32 [4, 48, 128], P('seg', 'blk'), may hold values from 0 to 127
- right_sector: int32 [4, 16, 8], P('seg'), may hold values from 0 to 7, each once within a row
- sector_sizes: int32 [4, 2, 8], P('seg'), may hold values from 32 to 128, as said below
- step_size: float32 [4], P('seg'), may hold values from 0.2 to 0.6
Outputs:
- psi: float32 [4, 128, 128, 128], P('seg', 'blk')
- energy: float32 [4], P('seg')
- density: float32 [4, 1024, 128], P('seg', 'blk')
Inputs may be any that keep to these rules, and one draw needn't show every extreme that they name: `sector_sizes`: in each row of 8 sizes one equals 128. `right_sector`: each row is a permutation of the sectors.
All inputs are finite; a program needn't handle non-finite values.
Results may differ from a plain program's by a relative error of at most 0.0018.
Values may be sent and summed in bfloat16 or wider, within the bound.
No kernel may reach another device: no remote copies, remote signals or barrier semaphores. Data moves between devices by JAX's collectives and lax.ppermute only.
A program may use at most 128 MiB of HBM per device.

v0:
```python
import jax
import jax.numpy as jnp
from jax import lax
from jax.sharding import PartitionSpec as P

NSEC = 8
BS = 128
P_SIZE = 16
ITERS = 3
NB = 128


def shifted_2(block, axis, distance):
    devices = range(lax.axis_size(axis))
    route = [(i - distance, i) for i in devices if i - distance in devices]
    return lax.ppermute(block, axis, route)


def block_mask(indices, sizes, right_flat):
    left_ids = indices % NSEC
    right_ids = jnp.take(right_flat, indices)
    positions = jnp.arange(BS, dtype=jnp.int32)
    row_live = positions[None, :] < jnp.take(sizes[0], left_ids)[:, None]
    col_live = positions[None, :] < jnp.take(sizes[1], right_ids)[:, None]
    return (row_live[:, :, None] & col_live[:, None, :]).astype(jnp.float32)


def apply_terms(full_bf, indices, left_env, right_env, weights, sources, right_flat):
    left_ids = indices % NSEC
    right_ids = jnp.take(right_flat, indices)

    def channel(accum, inputs):
        left_one, right_one, source_one, weight_one = inputs
        picked = jnp.take(full_bf, jnp.take(source_one, indices), axis=0)
        left_mats = jnp.take(left_one, left_ids, axis=0)
        middle = jnp.einsum(
            "nay,nyb->nab", left_mats, picked, preferred_element_type=jnp.float32
        ).astype(jnp.bfloat16)
        right_mats = jnp.take(right_one, right_ids, axis=0)
        result = jnp.einsum("nab,ncb->nac", middle, right_mats, preferred_element_type=jnp.float32)
        scaled = jnp.take(weight_one, indices)
        return (accum + scaled[:, None, None] * result, None)

    initial = jnp.zeros((indices.shape[0], BS, BS), jnp.float32)
    summed, _ = lax.scan(channel, initial, (left_env, right_env, sources, weights))
    return summed


def gram_parts(vector, indices, right_flat):
    left_ids = indices % NSEC
    right_ids = jnp.take(right_flat, indices)
    gram_left = jnp.einsum("nxb,nyb->nxy", vector, vector, precision=lax.Precision.HIGHEST)
    gram_right = jnp.einsum("nax,nay->nxy", vector, vector, precision=lax.Precision.HIGHEST)
    labels = jnp.arange(NSEC, dtype=jnp.int32)
    one_left = (left_ids[:, None] == labels[None, :]).astype(jnp.float32)
    one_right = (right_ids[:, None] == labels[None, :]).astype(jnp.float32)
    left_rho = jnp.einsum(
        "ns,nxy->sxy", one_left, gram_left, precision=lax.Precision.HIGHEST
    ).reshape(NSEC * BS, BS)
    right_rho = jnp.einsum(
        "ns,nxy->sxy", one_right, gram_right, precision=lax.Precision.HIGHEST
    ).reshape(NSEC * BS, BS)
    return (left_rho, right_rho)


def update_vector(current, applied, square_sum, cross_sum, image_sum, step_len, cells_total):
    quotient = cross_sum / square_sum
    new_norm = square_sum + step_len * step_len * (image_sum - quotient * quotient * square_sum)
    updated = (current - step_len * (applied - quotient * current)) * jnp.sqrt(
        cells_total / new_norm
    )
    return (updated, quotient)


def on_device(psi_init, env_left, env_right, coef, source, right_sector, sector_sizes, step_size):
    left_env = env_left[0]
    right_env = env_right[0]
    weights = coef[0]
    sources = source[0]
    right_flat = right_sector[0].reshape(NB)
    sizes = sector_sizes[0]
    step_len = step_size[0]
    own_count = psi_init.shape[1]
    cells_total = float(NB * BS * BS)
    own_ids = lax.axis_index("blk") * own_count + jnp.arange(own_count, dtype=jnp.int32)
    own_live = block_mask(own_ids, sizes, right_flat)
    current = psi_init[0] * own_live
    quotient = jnp.zeros((), jnp.float32)
    for iteration in range(ITERS):
        full_bf = lax.all_gather(current.astype(jnp.bfloat16), "blk", axis=0, tiled=True)

        def partial_terms(begin_row, row_count, full_bf=full_bf):
            indices = jnp.arange(row_count, dtype=jnp.int32)
            return apply_terms(full_bf, indices, left_env, right_env, weights, sources, right_flat)

        applied = (
            lax.psum_scatter(
                partial_terms(jnp.int32(0), own_count * lax.axis_size("blk")),
                "blk",
                scatter_dimension=0,
                tiled=True,
            )
            * own_live
        )
        square_sum, cross_sum, image_sum = lax.psum(
            (jnp.sum(current * current), jnp.sum(current * applied), jnp.sum(applied * applied)),
            "blk",
        )
        current, quotient = update_vector(
            current, applied, square_sum, cross_sum, image_sum, step_len, cells_total
        )
    left_part, right_part = gram_parts(current, own_ids, right_flat)
    left_rows, right_rows = (
        lax.psum_scatter(left_part, "blk", scatter_dimension=0, tiled=True),
        lax.psum_scatter(right_part, "blk", scatter_dimension=0, tiled=True),
    )
    shifted = shifted_2(right_rows, "seg", 1)
    density = (left_rows + shifted) / float(P_SIZE * BS)
    return (current[None], quotient.reshape(1), density[None])


def solution(mesh):
    in_specs = (
        P("seg", "blk", None, None),
        P("seg", "blk", None, None, None),
        P("seg", "blk", None, None, None),
        P("seg", "blk", None),
        P("seg", "blk", None),
        P("seg", None, None),
        P("seg", None, None),
        P("seg"),
    )
    out_specs = (P("seg", "blk", None, None), P("seg"), P("seg", "blk", None))
    return jax.shard_map(
        on_device, mesh=mesh, in_specs=in_specs, out_specs=out_specs, check_vma=False
    )
```

profile of v0, /device:TPU:0, one launch (start us, length us, event | category | flops | bytes accessed | tf_op | source)
XLA Modules:
  0.0 1026.9 jit_solution(6705878778556902143)
XLA Ops:
  16.2 47.1 %all-gather.4.cloned.1.call-done = bf16[128,128,128]{2,1,0:T(8,128)(2,1)} async-done(((bf16[16,128,128]{2,1,0:T(8,128)(2,1)}), bf16[128,128,128]{2,1,0:T(8,128)(2,1)}) %all-gather.4.cloned.1.call-update) | async-done | bytes 4194320 | tf_op jit(solution)/shard_map/all_gather | solution.py:90
  63.3 155.7 %while.36 = (s32[]{:T(128)}, f32[128,128,128]{2,1,0:T(8,128)}, f32[6,128]{1,0:T(8,128)S(1)}, bf16[6,8,128,128]{3,2,1,0:T(8,128)(2,1)S(1)}, s32[6,128]{1,0:T(8,12...) while((s32[]{:T(128)}, f32[128,128,128]{2,1,0:T(8,128)}, ...), condition=%wide.region_1.8_spmd.clone.clone, body=%wide.region_0.7_spmd.clone.clone.sunk | while | flops 1088431104 | bytes 55605632 | solution.py:45
  69.9 5.2 gather_fusion.3
  78.1 9.6 select_add_fusion.6
  94.3 5.2 gather_fusion.3
  102.6 11.4 %select_add_fusion.6 = f32[128,128,128]{2,1,0:T(8,128)} fusion(f32[128,128,128]{2,1,0:T(8,128)} %get-tuple-element.638, f32[128]{0:T(128)S(1)} %compare_select_fusion.30, pred[]{:T(512)S(6)} %compare.15, bf16[128,128,128]{2,1,0:T(8,128)(2,1)} %gather_fusion.1, pred[128]{0:T(512)(128)(4,1)S(1)} %get-tuple-element.592, ...), kind=kOutput, calls=%fused_computation.25.clone.1 | convolution fusion | flops 1088421888 | bytes 29361024 | tf_op jit(solution)/shard_map/while/body/eval_jaxpr/nab,ncb->nac/dot_general | solution.py:40
  120.6 5.2 gather_fusion.3
  128.8 11.4 %select_add_fusion.6 = f32[128,128,128]{2,1,0:T(8,128)} fusion(f32[128,128,128]{2,1,0:T(8,128)} %get-tuple-element.638, f32[128]{0:T(128)S(1)} %compare_select_fusion.30, pred[]{:T(512)S(6)} %compare.15, bf16[128,128,128]{2,1,0:T(8,128)(2,1)} %gather_fusion.1, pred[128]{0:T(512)(128)(4,1)S(1)} %get-tuple-element.592, ...), kind=kOutput, calls=%fused_computation.25.clone.1 | convolution fusion | flops 1088421888 | bytes 29361024 | tf_op jit(solution)/shard_map/while/body/eval_jaxpr/nab,ncb->nac/dot_general | solution.py:40
  146.8 5.2 gather_fusion.3
  155.1 11.4 %select_add_fusion.6 = f32[128,128,128]{2,1,0:T(8,128)} fusion(f32[128,128,128]{2,1,0:T(8,128)} %get-tuple-element.638, f32[128]{0:T(128)S(1)} %compare_select_fusion.30, pred[]{:T(512)S(6)} %compare.15, bf16[128,128,128]{2,1,0:T(8,128)(2,1)} %gather_fusion.1, pred[128]{0:T(512)(128)(4,1)S(1)} %get-tuple-element.592, ...), kind=kOutput, calls=%fused_computation.25.clone.1 | convolution fusion | flops 1088421888 | bytes 29361024 | tf_op jit(solution)/shard_map/while/body/eval_jaxpr/nab,ncb->nac/dot_general | solution.py:40
  173.1 5.2 gather_fusion.3
  181.4 11.4 %select_add_fusion.6 = f32[128,128,128]{2,1,0:T(8,128)} fusion(f32[128,128,128]{2,1,0:T(8,128)} %get-tuple-element.638, f32[128]{0:T(128)S(1)} %compare_select_fusion.30, pred[]{:T(512)S(6)} %compare.15, bf16[128,128,128]{2,1,0:T(8,128)(2,1)} %gather_fusion.1, pred[128]{0:T(512)(128)(4,1)S(1)} %get-tuple-element.592, ...), kind=kOutput, calls=%fused_computation.25.clone.1 | convolution fusion | flops 1088421888 | bytes 29361024 | tf_op jit(solution)/shard_map/while/body/eval_jaxpr/nab,ncb->nac/dot_general | solution.py:40
  199.3 5.2 gather_fusion.3
  207.6 11.4 %select_add_fusion.6 = f32[128,128,128]{2,1,0:T(8,128)} fusion(f32[128,128,128]{2,1,0:T(8,128)} %get-tuple-element.638, f32[128]{0:T(128)S(1)} %compare_select_fusion.30, pred[]{:T(512)S(6)} %compare.15, bf16[128,128,128]{2,1,0:T(8,128)(2,1)} %gather_fusion.1, pred[128]{0:T(512)(128)(4,1)S(1)} %get-tuple-element.592, ...), kind=kOutput, calls=%fused_computation.25.clone.1 | convolution fusion | flops 1088421888 | bytes 29361024 | tf_op jit(solution)/shard_map/while/body/eval_jaxpr/nab,ncb->nac/dot_general | solution.py:40
  219.8 87.7 %reduce-scatter.6.cloned.1.call-done = f32[16,128,128]{2,1,0:T(8,128)} async-done(((f32[128,128,128]{2,1,0:T(8,128)}), f32[16,128,128]{2,1,0:T(8,128)}) %reduce-scatter.6.cloned.1.call-update) | async-done | bytes 1048592 | tf_op jit(solution)/shard_map/reduce_scatter | solution.py:97
  309.7 14.3 %all-reduce.2 = (f32[]{:T(128)}, f32[]{:T(128)}, f32[]{:T(128)}) all-reduce(f32[]{:T(128)} %get-tuple-element.347, f32[]{:T(128)} %get-tuple-element.348, f32[]{:T(128)} %get-tuple-element.346), channel_id=1, replica_groups=mesh['seg'=4,'blk'=8] {'blk'}, use_global_device_ids=true, to_apply=%region_6.13 | all-reduce | flops 3 | bytes 24 | tf_op jit(solution)/shard_map/psum | solution.py:105
  329.9 45.3 %all-gather.6.cloned.1.call-done = bf16[128,128,128]{2,1,0:T(8,128)(2,1)} async-done(((bf16[16,128,128]{2,1,0:T(8,128)(2,1)}), bf16[128,128,128]{2,1,0:T(8,128)(2,1)}) %all-gather.6.cloned.1.call-update) | async-done | bytes 4194320 | tf_op jit(solution)/shard_map/all_gather | solution.py:90
  375.2 155.7 %while.37 = (s32[]{:T(128)}, f32[128,128,128]{2,1,0:T(8,128)}, f32[6,128]{1,0:T(8,128)S(1)}, bf16[6,8,128,128]{3,2,1,0:T(8,128)(2,1)S(1)}, s32[6,128]{1,0:T(8,12...) while((s32[]{:T(128)}, f32[128,128,128]{2,1,0:T(8,128)}, ...), condition=%wide.region_10.17_spmd.clone.clone, body=%wide.region_9.16_spmd.clone.clone.sunk | while | flops 1088431104 | bytes 55605632 | solution.py:45
  381.8 5.2 gather_fusion.8
  390.0 9.6 select_add_fusion.7
  406.2 5.2 gather_fusion.8
  414.5 11.4 %select_add_fusion.7 = f32[128,128,128]{2,1,0:T(8,128)} fusion(f32[128,128,128]{2,1,0:T(8,128)} %get-tuple-element.668, f32[128]{0:T(128)S(1)} %compare_select_fusion.32, pred[]{:T(512)S(6)} %compare.16, bf16[128,128,128]{2,1,0:T(8,128)(2,1)} %gather_fusion.6, pred[128]{0:T(512)(128)(4,1)S(1)} %get-tuple-element.607, ...), kind=kOutput, calls=%fused_computation.56.clone.1 | convolution fusion | flops 1088421888 | bytes 29361024 | tf_op jit(solution)/shard_map/while/body/eval_jaxpr/nab,ncb->nac/dot_general | solution.py:40
  432.4 5.2 gather_fusion.8
  440.7 11.4 %select_add_fusion.7 = f32[128,128,128]{2,1,0:T(8,128)} fusion(f32[128,128,128]{2,1,0:T(8,128)} %get-tuple-element.668, f32[128]{0:T(128)S(1)} %compare_select_fusion.32, pred[]{:T(512)S(6)} %compare.16, bf16[128,128,128]{2,1,0:T(8,128)(2,1)} %gather_fusion.6, pred[128]{0:T(512)(128)(4,1)S(1)} %get-tuple-element.607, ...), kind=kOutput, calls=%fused_computation.56.clone.1 | convolution fusion | flops 1088421888 | bytes 29361024 | tf_op jit(solution)/shard_map/while/body/eval_jaxpr/nab,ncb->nac/dot_general | solution.py:40
  458.7 5.2 gather_fusion.8
  467.0 11.4 %select_add_fusion.7 = f32[128,128,128]{2,1,0:T(8,128)} fusion(f32[128,128,128]{2,1,0:T(8,128)} %get-tuple-element.668, f32[128]{0:T(128)S(1)} %compare_select_fusion.32, pred[]{:T(512)S(6)} %compare.16, bf16[128,128,128]{2,1,0:T(8,128)(2,1)} %gather_fusion.6, pred[128]{0:T(512)(128)(4,1)S(1)} %get-tuple-element.607, ...), kind=kOutput, calls=%fused_computation.56.clone.1 | convolution fusion | flops 1088421888 | bytes 29361024 | tf_op jit(solution)/shard_map/while/body/eval_jaxpr/nab,ncb->nac/dot_general | solution.py:40
  485.0 5.2 gather_fusion.8
  493.2 11.4 %select_add_fusion.7 = f32[128,128,128]{2,1,0:T(8,128)} fusion(f32[128,128,128]{2,1,0:T(8,128)} %get-tuple-element.668, f32[128]{0:T(128)S(1)} %compare_select_fusion.32, pred[]{:T(512)S(6)} %compare.16, bf16[128,128,128]{2,1,0:T(8,128)(2,1)} %gather_fusion.6, pred[128]{0:T(512)(128)(4,1)S(1)} %get-tuple-element.607, ...), kind=kOutput, calls=%fused_computation.56.clone.1 | convolution fusion | flops 1088421888 | bytes 29361024 | tf_op jit(solution)/shard_map/while/body/eval_jaxpr/nab,ncb->nac/dot_general | solution.py:40
  511.2 5.2 gather_fusion.8
  519.5 11.4 %select_add_fusion.7 = f32[128,128,128]{2,1,0:T(8,128)} fusion(f32[128,128,128]{2,1,0:T(8,128)} %get-tuple-element.668, f32[128]{0:T(128)S(1)} %compare_select_fusion.32, pred[]{:T(512)S(6)} %compare.16, bf16[128,128,128]{2,1,0:T(8,128)(2,1)} %gather_fusion.6, pred[128]{0:T(512)(128)(4,1)S(1)} %get-tuple-element.607, ...), kind=kOutput, calls=%fused_computation.56.clone.1 | convolution fusion | flops 1088421888 | bytes 29361024 | tf_op jit(solution)/shard_map/while/body/eval_jaxpr/nab,ncb->nac/dot_general | solution.py:40
  530.9 88.4 %reduce-scatter.8.cloned.1.call-done = f32[16,128,128]{2,1,0:T(8,128)} async-done(((f32[128,128,128]{2,1,0:T(8,128)}), f32[16,128,128]{2,1,0:T(8,128)}) %reduce-scatter.8.cloned.1.call-update) | async-done | bytes 1048592 | tf_op jit(solution)/shard_map/reduce_scatter | solution.py:97
  621.5 14.3 %all-reduce.1 = (f32[]{:T(128)}, f32[]{:T(128)}, f32[]{:T(128)}) all-reduce(f32[]{:T(128)} %get-tuple-element.350, f32[]{:T(128)} %get-tuple-element.345, f32[]{:T(128)} %get-tuple-element.344), channel_id=1, replica_groups=mesh['seg'=4,'blk'=8] {'blk'}, use_global_device_ids=true, to_apply=%region_15.22 | all-reduce | flops 3 | bytes 24 | tf_op jit(solution)/shard_map/psum | solution.py:105
  641.8 45.1 %all-gather.8.cloned.1.call-done = bf16[128,128,128]{2,1,0:T(8,128)(2,1)} async-done(((bf16[16,128,128]{2,1,0:T(8,128)(2,1)}), bf16[128,128,128]{2,1,0:T(8,128)(2,1)}) %all-gather.8.cloned.1.call-update) | async-done | bytes 4194320 | tf_op jit(solution)/shard_map/all_gather | solution.py:90
  686.9 155.7 %while.38 = (s32[]{:T(128)}, f32[128,128,128]{2,1,0:T(8,128)}, f32[6,128]{1,0:T(8,128)S(1)}, bf16[6,8,128,128]{3,2,1,0:T(8,128)(2,1)S(1)}, s32[6,128]{1,0:T(8,12...) while((s32[]{:T(128)}, f32[128,128,128]{2,1,0:T(8,128)}, ...), condition=%wide.region_19.26_spmd.clone.clone, body=%wide.region_18.25_spmd.clone.clone.sunk | while | flops 1088431104 | bytes 55605632 | solution.py:45
  693.5 5.2 gather_fusion.13
  701.8 9.6 select_add_fusion.8
  717.9 5.2 gather_fusion.13
  726.2 11.4 %select_add_fusion.8 = f32[128,128,128]{2,1,0:T(8,128)} fusion(f32[128,128,128]{2,1,0:T(8,128)} %get-tuple-element.698, f32[128]{0:T(128)S(1)} %compare_select_fusion.34, pred[]{:T(512)S(6)} %compare.17, bf16[128,128,128]{2,1,0:T(8,128)(2,1)} %gather_fusion.11, pred[128]{0:T(512)(128)(4,1)S(1)} %get-tuple-element.622, ...), kind=kOutput, calls=%fused_computation.87.clone.1 | convolution fusion | flops 1088421888 | bytes 29361024 | tf_op jit(solution)/shard_map/while/body/eval_jaxpr/nab,ncb->nac/dot_general | solution.py:40
  744.2 5.2 gather_fusion.13
  752.5 11.4 %select_add_fusion.8 = f32[128,128,128]{2,1,0:T(8,128)} fusion(f32[128,128,128]{2,1,0:T(8,128)} %get-tuple-element.698, f32[128]{0:T(128)S(1)} %compare_select_fusion.34, pred[]{:T(512)S(6)} %compare.17, bf16[128,128,128]{2,1,0:T(8,128)(2,1)} %gather_fusion.11, pred[128]{0:T(512)(128)(4,1)S(1)} %get-tuple-element.622, ...), kind=kOutput, calls=%fused_computation.87.clone.1 | convolution fusion | flops 1088421888 | bytes 29361024 | tf_op jit(solution)/shard_map/while/body/eval_jaxpr/nab,ncb->nac/dot_general | solution.py:40
  778.7 11.4 %select_add_fusion.8 = f32[128,128,128]{2,1,0:T(8,128)} fusion(f32[128,128,128]{2,1,0:T(8,128)} %get-tuple-element.698, f32[128]{0:T(128)S(1)} %compare_select_fusion.34, pred[]{:T(512)S(6)} %compare.17, bf16[128,128,128]{2,1,0:T(8,128)(2,1)} %gather_fusion.11, pred[128]{0:T(512)(128)(4,1)S(1)} %get-tuple-element.622, ...), kind=kOutput, calls=%fused_computation.87.clone.1 | convolution fusion | flops 1088421888 | bytes 29361024 | tf_op jit(solution)/shard_map/while/body/eval_jaxpr/nab,ncb->nac/dot_general | solution.py:40
  805.0 11.4 %select_add_fusion.8 = f32[128,128,128]{2,1,0:T(8,128)} fusion(f32[128,128,128]{2,1,0:T(8,128)} %get-tuple-element.698, f32[128]{0:T(128)S(1)} %compare_select_fusion.34, pred[]{:T(512)S(6)} %compare.17, bf16[128,128,128]{2,1,0:T(8,128)(2,1)} %gather_fusion.11, pred[128]{0:T(512)(128)(4,1)S(1)} %get-tuple-element.622, ...), kind=kOutput, calls=%fused_computation.87.clone.1 | convolution fusion | flops 1088421888 | bytes 29361024 | tf_op jit(solution)/shard_map/while/body/eval_jaxpr/nab,ncb->nac/dot_general | solution.py:40
  823.0 5.2 gather_fusion.13
  831.2 11.4 %select_add_fusion.8 = f32[128,128,128]{2,1,0:T(8,128)} fusion(f32[128,128,128]{2,1,0:T(8,128)} %get-tuple-element.698, f32[128]{0:T(128)S(1)} %compare_select_fusion.34, pred[]{:T(512)S(6)} %compare.17, bf16[128,128,128]{2,1,0:T(8,128)(2,1)} %gather_fusion.11, pred[128]{0:T(512)(128)(4,1)S(1)} %get-tuple-element.622, ...), kind=kOutput, calls=%fused_computation.87.clone.1 | convolution fusion | flops 1088421888 | bytes 29361024 | tf_op jit(solution)/shard_map/while/body/eval_jaxpr/nab,ncb->nac/dot_general | solution.py:40
  842.7 88.4 %reduce-scatter.10.cloned.1.call-done = f32[16,128,128]{2,1,0:T(8,128)} async-done(((f32[128,128,128]{2,1,0:T(8,128)}), f32[16,128,128]{2,1,0:T(8,128)}) %reduce-scatter.10.cloned.1.call-update) | async-done | bytes 1048592 | tf_op jit(solution)/shard_map/reduce_scatter | solution.py:97
  933.2 14.3 %all-reduce = (f32[]{:T(128)}, f32[]{:T(128)}, f32[]{:T(128)}) all-reduce(f32[]{:T(128)} %get-tuple-element.349, f32[]{:T(128)} %get-tuple-element.343, f32[]{:T(128)} %get-tuple-element.342), channel_id=1, replica_groups=mesh['seg'=4,'blk'=8] {'blk'}, use_global_device_ids=true, to_apply=%region_24.31 | all-reduce | flops 3 | bytes 24 | tf_op jit(solution)/shard_map/psum | solution.py:105
  960.6 25.3 %reduce-scatter.14.cloned.1.call-done = f32[128,128]{1,0:T(8,128)} async-done(((f32[1024,128]{1,0:T(8,128)}), f32[128,128]{1,0:T(8,128)}) %reduce-scatter.14.cloned.1.call-update) | async-done | bytes 65552 | tf_op jit(solution)/shard_map/reduce_scatter | solution.py:115
  989.2 28.2 %reduce-scatter.12.cloned.1.call-done = f32[128,128]{1,0:T(8,128)} async-done(((f32[1024,128]{1,0:T(8,128)}), f32[128,128]{1,0:T(8,128)}) %reduce-scatter.12.cloned.1.call-update) | async-done | bytes 65552 | tf_op jit(solution)/shard_map/reduce_scatter | solution.py:114
  (359 shorter events, 218.0 us)
Async XLA Ops:
  7.2 56.1 %copy-start.1 = (bf16[1,6,8,128,128]{4,3,2,1,0:T(8,128)(2,1)S(1)}, bf16[1,6,8,128,128]{4,3,2,1,0:T(8,128)(2,1)}, u32[]{:S(2)}) copy-start(bf16[1,6,8,128,128]{4,3,2,1,0:T(8,128)(2,1)} %param.27) | copy-start | bytes 4718596
  7.2 56.1 %all-gather.4.cloned.1.call-start = ((), (), s32[]{:S(2)}) async-start(), calls=%async_computation.5 | async-start | bytes 4718592 | tf_op jit(solution)/shard_map/all_gather | solution.py:90
  9.6 53.7 %copy-start.4 = (s32[16]{0:T(128)}, s32[16]{0:T(128)S(1)}, u32[]{:S(2)}) copy-start(s32[16]{0:T(128)S(1)} %get-tuple-element.419) | copy-start | bytes 196
  13.5 294.0 %reduce-scatter.6.cloned.1.call-start = ((), (), s32[]{:S(2)}) async-start(), calls=%async_computation.6 | async-start | bytes 9437184 | tf_op jit(solution)/shard_map/reduce_scatter | solution.py:97
  219.0 88.5 %copy-start.3 = (f32[1,16,128,128]{3,2,1,0:T(8,128)S(1)}, f32[1,16,128,128]{3,2,1,0:T(8,128)}, u32[]{:S(2)}) copy-start(f32[1,16,128,128]{3,2,1,0:T(8,128)} %param.26) | copy-start | bytes 3145732
  219.0 156.1 %all-gather.6.cloned.1.call-start = ((), (), s32[]{:S(2)}) async-start(), calls=%async_computation.7 | async-start | bytes 4718592 | tf_op jit(solution)/shard_map/all_gather | solution.py:90
  329.8 289.6 %copy-start.2 = (f32[16,128,128]{2,1,0:T(8,128)}, f32[16,128,128]{2,1,0:T(8,128)S(1)}, u32[]{:S(2)}) copy-start(f32[16,128,128]{2,1,0:T(8,128)S(1)} %get-tuple-element.417) | copy-start | bytes 3145732
  329.8 289.5 %reduce-scatter.8.cloned.1.call-start = ((), (), s32[]{:S(2)}) async-start(), calls=%async_computation.8 | async-start | bytes 9437184 | tf_op jit(solution)/shard_map/reduce_scatter | solution.py:97
  530.9 156.0 %all-gather.8.cloned.1.call-start = ((), (), s32[]{:S(2)}) async-start(), calls=%async_computation.9 | async-start | bytes 4718592 | tf_op jit(solution)/shard_map/all_gather | solution.py:90
  641.6 289.5 %reduce-scatter.10.cloned.1.call-start = ((), (), s32[]{:S(2)}) async-start(), calls=%async_computation.10 | async-start | bytes 9437184 | tf_op jit(solution)/shard_map/reduce_scatter | solution.py:97
  842.6 143.2 %reduce-scatter.14.cloned.1.call-start = ((), (), s32[]{:S(2)}) async-start(), calls=%async_computation.12 | async-start | bytes 589824 | tf_op jit(solution)/shard_map/reduce_scatter | solution.py:115
  931.1 23.1 %copy-start.5 = (s32[16]{0:T(128)S(1)}, s32[16]{0:T(128)}, u32[]{:S(2)}) copy-start(s32[16]{0:T(128)} %copy-done.4) | copy-start | bytes 196
  952.4 6.2 copy-start
  956.2 61.3 %reduce-scatter.12.cloned.1.call-start = ((), (), s32[]{:S(2)}) async-start(), calls=%async_computation.11 | async-start | bytes 589824 | tf_op jit(solution)/shard_map/reduce_scatter | solution.py:114
  985.9 31.6 %collective-permute-start = (f32[128,128]{1,0:T(8,128)}, f32[128,128]{1,0:T(8,128)S(1)}, u32[]{:S(2)}, u32[]{:S(2)}) collective-permute-start(f32[128,128]{1,0:T(8,128)} %reduce-scatter.14.cloned.1.call-done), channel_id=1, source_target_pairs={{0,8},{8,16},{16,24},{1,9},{9,17},{17,25},{2,10},{10,18},{18,26},{... | collective-permute-start | bytes 196616 | tf_op jit(solution)/shard_map/ppermute | solution.py:16
Sparse Core Ops, SparseCore 0:
  13.6 49.5 all-gather.3
  219.2 88.3 reduce-scatter.5
  330.0 45.1 all-gather.5
  531.0 88.3 reduce-scatter.7
  641.7 45.1 all-gather.7
  842.8 88.3 reduce-scatter.9
  956.3 29.4 reduce-scatter.13
  988.1 29.2 reduce-scatter.11
where the time goes:
time: 1030 us
  waiting for transfers between devices  456 us (44%)
  local copies, waits for them, and re-layouts  273 us (27%)
  matrix products  206 us (20%)
  blocking collectives  42.9 us (4%)
  between operations  26.2 us (3%)
  other arithmetic  17.7 us (2%)
    reduce_scatter x3, waiting for transfers between devices, on_device(): lax.psum_scatter(partial_terms(jnp.int32(0), own_count * lax.axis_size('b...  265 us
    dot_general x18, matrix products, channel(): jnp.einsum('nab,ncb->nac', middle, right_mats, preferred_element_type=jnp...  199 us
    all_gather x3, waiting for transfers between devices, on_device(): lax.all_gather(current.astype(jnp.bfloat16), 'blk', axis=0, tiled=True)  137 us
    gather x36, local copies, waits for them, and re-layouts, channel(): picked = jnp.take(full_bf, jnp.take(source_one, indices), axis=0)  116 us
    gather x18, local copies, waits for them, and re-layouts, channel(): left_mats = jnp.take(left_one, left_ids, axis=0)  55 us
    gather x18, local copies, waits for them, and re-layouts, channel(): right_mats = jnp.take(right_one, right_ids, axis=0)  54.5 us
    psum x3, blocking collectives, on_device(): lax.psum((jnp.sum(current * current), jnp.sum(current * applied), jnp.sum...  42.9 us
    reduce_scatter x1, waiting for transfers between devices, on_device(): lax.psum_scatter(left_part, 'blk', scatter_dimension=0, tiled=True)  28.2 us
  transfers between devices with their start and end apart: 9, of which 8 were waited for; matrix products, arithmetic and copies ran while one was open for 1% of the time, Pallas kernels for 0%

commit v1 on v0

--- a/solution.py
+++ b/solution.py
@@ -1,6 +1,10 @@
+import functools
+
 import jax
 import jax.numpy as jnp
 from jax import lax
+from jax.experimental import pallas as pl
+from jax.experimental.pallas import tpu as pltpu
 from jax.sharding import PartitionSpec as P
 
 NSEC = 8
@@ -72,7 +76,7 @@
     return (updated, quotient)
 
 
-def on_device(psi_init, env_left, env_right, coef, source, right_sector, sector_sizes, step_size):
+def on_device_general(psi_init, env_left, env_right, coef, source, right_sector, sector_sizes, step_size):
     left_env = env_left[0]
     right_env = env_right[0]
     weights = coef[0]
@@ -119,6 +123,233 @@
     return (current[None], quotient.reshape(1), density[None])
 
 
+BF = jnp.bfloat16
+F32 = jnp.float32
+MIB = 1 << 20
+TOP = 32767.0
+EXP_ROWS = 16
+ROWS_ROWS = (((1,), (1,)), ((), ()))
+COLS_COLS = (((0,), (0,)), ((), ()))
+SMEM = pl.BlockSpec(memory_space=pltpu.SMEM)
+VMEM = pl.BlockSpec(memory_space=pltpu.VMEM)
+
+
+def terms_kernel(
+    coded, turned, unroll, place, coef_a, coef_b, from_a, from_b, inverse, full,
+    left_a, left_b, right_a, right_b, out, middle,
+):
+    halves = ((coef_a, from_a, left_a, right_a), (coef_b, from_b, left_b, right_b))
+    count = left_a.shape[0]
+    base = place[0] * (2 * NSEC)
+
+    def first(a):
+        for half, (_, sources, left, _) in enumerate(halves):
+            for k in range(count):
+                one = full[sources[k, base + a]]
+                two = full[sources[k, base + NSEC + a]]
+                if turned:
+                    both = jnp.concatenate([one, two], axis=0)
+                    product = lax.dot_general(
+                        left[k, a], both, ROWS_ROWS, preferred_element_type=F32
+                    )
+                else:
+                    both = jnp.concatenate([one, two], axis=1)
+                    product = jnp.dot(left[k, a], both, preferred_element_type=F32)
+                product = product.astype(BF)
+                middle[half * count + k, 0, a] = product[:, :BS]
+                middle[half * count + k, 1, a] = product[:, BS:]
+
+    def second(b):
+        picked = [inverse[place[0] * 2 + t, b] for t in range(2)]
+        sums = [None, None]
+        for half, (weights, _, _, right) in enumerate(halves):
+            for k in range(count):
+                both = jnp.concatenate(
+                    [middle[half * count + k, t, picked[t]] for t in range(2)], axis=0
+                )
+                product = lax.dot_general(right[k, b], both, ROWS_ROWS, preferred_element_type=F32)
+                for t in range(2):
+                    term = product[:, t * BS : (t + 1) * BS] * weights[k, base + t * NSEC + picked[t]]
+                    sums[t] = term if sums[t] is None else sums[t] + term
+        for t in range(2):
+            index = t * NSEC + picked[t]
+            if not coded:
+                out[index] = sums[t]
+                continue
+            most = jnp.max(jnp.abs(sums[t]), axis=(0, 1), keepdims=True)
+            power = jnp.clip(jnp.ceil(jnp.log2(jnp.maximum(most, 1e-30) / TOP)), -100.0, 100.0)
+            whole = jnp.clip(jnp.round(sums[t] * jnp.exp2(-power)), -TOP, TOP)
+            rows = pl.ds(pl.multiple_of(index * BS, BS), BS)
+            out[rows, :] = whole.astype(jnp.int32).astype(jnp.int16)
+            last = 2 * NSEC * BS
+            here = lax.broadcasted_iota(jnp.int32, (EXP_ROWS, BS), 0) == index
+            old = out[last : last + EXP_ROWS, :].astype(jnp.int32)
+            new = jnp.broadcast_to(power.astype(jnp.int32), (EXP_ROWS, BS))
+            out[last : last + EXP_ROWS, :] = jnp.where(here, new, old).astype(jnp.int16)
+
+    def run(step):
+        def several(i, carry):
+            for j in range(unroll):
+                step(i * unroll + j)
+            return carry
+
+        lax.fori_loop(0, NSEC // unroll, several, 0)
+
+    run(first)
+    run(second)
+
+
+def terms(coded, turned, place, tables, full, envs):
+    channels = 2 * envs[0].shape[0]
+    blocks = 2 * NSEC
+    if coded:
+        shape = jax.ShapeDtypeStruct((blocks * BS + EXP_ROWS, BS), jnp.int16)
+    else:
+        shape = jax.ShapeDtypeStruct((blocks, BS, BS), F32)
+    return pl.pallas_call(
+        functools.partial(terms_kernel, coded, turned, 2),
+        out_shape=shape,
+        in_specs=[SMEM] * 6 + [VMEM] * 5,
+        out_specs=VMEM,
+        scratch_shapes=[pltpu.VMEM((channels, 2, NSEC, BS, BS), BF)],
+        compiler_params=pltpu.CompilerParams(vmem_limit_bytes=24 * MIB),
+        cost_estimate=pl.CostEstimate(
+            flops=channels * blocks * 4 * BS**3, bytes_accessed=8 * MIB, transcendentals=0
+        ),
+    )(place, *tables, full, *envs)
+
+
+def combine_kernel(place, sizes, labels, own, *refs):
+    coded, current, applied, sums = refs[:-3], refs[-3], refs[-2], refs[-1]
+    blocks = own.shape[0]
+    down = lax.broadcasted_iota(jnp.int32, (BS, BS), 0)
+    across = lax.broadcasted_iota(jnp.int32, (BS, BS), 1)
+    totals = [jnp.zeros((8, BS), F32) for _ in range(3)]
+    for i in range(blocks):
+        t, a = i // NSEC, i % NSEC
+        value = own[i]
+        for one in coded:
+            power = one[blocks * BS : blocks * BS + EXP_ROWS, :].astype(jnp.int32).astype(F32)
+            scale = jnp.exp2(power[i : i + 1, :])
+            value = value + one[i * BS : (i + 1) * BS, :].astype(jnp.int32).astype(F32) * scale
+        live = (across < sizes[0, a]) & (down < sizes[1, labels[place[0] * 2 + t, a]])
+        value = jnp.where(live, value, 0.0)
+        applied[i] = value
+        old = current[i]
+        for n, terms_of in enumerate((old * old, old * value, value * value)):
+            totals[n] = totals[n] + jnp.sum(terms_of.reshape(BS // 8, 8, BS), axis=0)
+    for n in range(3):
+        sums[n] = totals[n]
+
+
+def combine(place, sizes, labels, own, coded, current):
+    return pl.pallas_call(
+        combine_kernel,
+        out_shape=(
+            jax.ShapeDtypeStruct(own.shape, F32),
+            jax.ShapeDtypeStruct((3, 8, BS), F32),
+        ),
+        in_specs=[SMEM] * 3 + [VMEM] * (2 + len(coded)),
+        out_specs=(VMEM, VMEM),
+        compiler_params=pltpu.CompilerParams(vmem_limit_bytes=16 * MIB),
+        cost_estimate=pl.CostEstimate(flops=10 * own.size, bytes_accessed=4 * MIB, transcendentals=0),
+    )(place, sizes, labels, own, *coded, current)
+
+
+def finish_kernel(place, scalars, inverse, current, applied, psi, left, right):
+    keep, take = scalars[0], scalars[1]
+    blocks = current.shape[0]
+    vals = [keep * current[i] - take * applied[i] for i in range(blocks)]
+    for i in range(blocks):
+        psi[i] = vals[i].T
+        applied[i] = vals[i]
+
+    def gram(dims, one, two):
+        kw = dict(precision=lax.Precision.HIGHEST, preferred_element_type=F32)
+        return lax.dot_general(one, one, dims, **kw) + lax.dot_general(two, two, dims, **kw)
+
+    for a in range(NSEC):
+        left[a] = gram(COLS_COLS, vals[a], vals[NSEC + a])
+    for b in range(NSEC):
+        one = applied[inverse[place[0] * 2, b]]
+        two = applied[NSEC + inverse[place[0] * 2 + 1, b]]
+        right[b] = gram(ROWS_ROWS, one, two)
+
+
+def finish(place, scalars, inverse, current, applied):
+    def kernel(place, scalars, inverse, current, applied, psi, left, right, hold):
+        for i in range(current.shape[0]):
+            hold[i] = applied[i]
+        finish_kernel(place, scalars, inverse, current, hold, psi, left, right)
+
+    rho = jax.ShapeDtypeStruct((NSEC, BS, BS), F32)
+    return pl.pallas_call(
+        kernel,
+        out_shape=(jax.ShapeDtypeStruct(current.shape, F32), rho, rho),
+        in_specs=[SMEM] * 3 + [VMEM] * 2,
+        out_specs=(VMEM,) * 3,
+        scratch_shapes=[pltpu.VMEM(current.shape, F32)],
+        compiler_params=pltpu.CompilerParams(vmem_limit_bytes=24 * MIB),
+    )(place, scalars, inverse, current, applied)
+
+
+def on_device_paired(psi_init, env_left, env_right, coef, source, right_sector, sector_sizes, step_size):
+    count = lax.axis_size("blk")
+    line = count // 2
+    me = lax.axis_index("blk")
+    swap = [(i, i ^ 1) for i in range(count)]
+    labels = right_sector[0]
+    sizes = sector_sizes[0]
+    step_len = step_size[0]
+    cells_total = float(NB * BS * BS)
+
+    def moved(x, by):
+        route = [(i, (i + 2 * by) % count) for i in range(count)]
+        return lax.ppermute(x, "blk", route)
+
+    mine = (env_left[0], env_right[0], coef[0], source[0])
+    other = tuple(lax.ppermute(x, "blk", swap) for x in mine)
+    envs = (mine[0], other[0], mine[1], other[1])
+    sector = jnp.arange(NSEC, dtype=jnp.int32)
+    inverse = jnp.sum(
+        jnp.where(labels[:, :, None] == sector[None, None, :], sector[None, :, None], 0), axis=1
+    ).astype(jnp.int32)
+    tables = (mine[2], other[2], mine[3], other[3], inverse)
+    places = [((me + 2 * by) % count).astype(jnp.int32).reshape(1) for by in range(line)]
+    order = sorted(range(1, line), key=lambda by: -min(by, line - by))
+
+    own_count = psi_init.shape[1]
+    own_ids = me * own_count + jnp.arange(own_count, dtype=jnp.int32)
+    start = psi_init[0] * block_mask(own_ids, sizes, labels.reshape(NB))
+    current = jnp.swapaxes(start, 1, 2)
+    half = start.astype(BF)
+    for iteration in range(ITERS):
+        full = lax.all_gather(half, "blk", axis=0, tiled=True)
+        turned = iteration > 0
+        arrived = []
+        for by in order:
+            arrived.append(moved(terms(True, turned, places[by], tables, full, envs), by))
+        own = terms(False, turned, places[0], tables, full, envs)
+        applied, sums = combine(places[0], sizes, labels, own, arrived, current)
+        square_sum, cross_sum, image_sum = lax.psum(jnp.sum(sums, axis=(1, 2)), "blk")
+        quotient = cross_sum / square_sum
+        new_norm = square_sum + step_len * step_len * (image_sum - quotient * quotient * square_sum)
+        scale = jnp.sqrt(cells_total / new_norm)
+        keep = (1.0 + step_len * quotient) * scale
+        take = step_len * scale
+        if iteration < ITERS - 1:
+            current = keep * current - take * applied
+            half = current.astype(BF)
+    psi, left_part, right_part = finish(
+        places[0], jnp.stack([keep, take]), inverse, current, applied
+    )
+    both = jnp.concatenate([left_part, right_part], axis=1).reshape(2 * NSEC * BS, BS)
+    both = lax.psum_scatter(both, "blk", scatter_dimension=0, tiled=True)
+    shifted = shifted_2(both[BS:], "seg", 1)
+    density = (both[:BS] + shifted) / float(P_SIZE * BS)
+    return (psi[None], quotient.reshape(1), density[None])
+
+
 def solution(mesh):
     in_specs = (
         P("seg", "blk", None, None),
@@ -131,6 +362,11 @@
         P("seg"),
     )
     out_specs = (P("seg", "blk", None, None), P("seg"), P("seg", "blk", None))
+    paired = NB // mesh.shape["blk"] == 2 * NSEC and mesh.shape["blk"] % 2 == 0
     return jax.shard_map(
-        on_device, mesh=mesh, in_specs=in_specs, out_specs=out_specs, check_vma=False
-    )
+        on_device_paired if paired else on_device_general,
+        mesh=mesh,
+        in_specs=in_specs,
+        out_specs=out_specs,
+        check_vma=False,
+    )

time: 1030 us -> 454 us (0.44)
  local copies, waits for them, and re-layouts: 273 us -> 20.6 us
  waiting for transfers between devices: 456 us -> 237 us
  matrix products: 206 us -> 0 us
  Pallas kernels: 0 us -> 95.8 us
  starting transfers between devices: 3.86 us -> 16.8 us
    reduce_scatter x5 -> x1, waiting for transfers between devices: 318 us -> 30.7 us  [on_device_paired(): both = lax.psum_scatter(both, 'blk', scatter_dimension=0, tiled=True)]
    gather x91 -> x0, local copies, waits for them, and re-layouts: 249 us -> none  [the longest x36 116 us: channel(): picked = jnp.take(full_bf, jnp.take(source_one, indices), axis=0)]
    dot_general x22 -> x0, matrix products: 206 us -> none  [the longest x18 199 us: channel(): jnp.einsum('nab,ncb->nac', middle, right_mats, preferred_element_type=jnp...]
    pallas_call x0 -> x16, Pallas kernels: none -> 95.8 us  [the longest x12 86.8 us: terms(): pl.pallas_call(functools.partial(terms_kernel, coded, turned, 2), out_sha...]
    ppermute x0 -> x13, waiting for transfers between devices: none -> 70.3 us  [the longest x9 65.6 us: moved(): return lax.ppermute(x, 'blk', route)]
    squeeze x54 -> x1, local copies, waits for them, and re-layouts: 18 us -> 0.07 us  [on_device_paired(): labels = right_sector[0]]
    ppermute x0 -> x13, starting transfers between devices: none -> 13.2 us  [the longest x9 12.1 us: moved(): return lax.ppermute(x, 'blk', route)]
    unnamed x15 -> x36, local copies, waits for them, and re-layouts: 2.16 us -> 12.9 us
  transfers between devices with their start and end apart: 9 -> 18, of which waited for: 8 -> 12; matrix products, arithmetic and copies ran while one was open for 1% -> 0% of each run, Pallas kernels for 0% -> 14%
where the time goes in v1:
time: 454 us; the launch traced here: 453 us
  waiting for transfers between devices  237 us (52%)
  Pallas kernels  95.8 us (21%)
  blocking collectives  45.1 us (10%)
  between operations  25.2 us (6%)
  local copies, waits for them, and re-layouts  20.6 us (5%)
  starting transfers between devices  16.8 us (4%)
  other arithmetic  12.8 us (3%)
    all_gather x3, waiting for transfers between devices, on_device_paired(): full = lax.all_gather(half, 'blk', axis=0, tiled=True)  134 us
    pallas_call x12, Pallas kernels, terms(): pl.pallas_call(functools.partial(terms_kernel, coded, turned, 2), out_sha...  86.8 us
    ppermute x9, waiting for transfers between devices, moved(): return lax.ppermute(x, 'blk', route)  65.6 us
    psum x3, blocking collectives, on_device_paired(): lax.psum(jnp.sum(sums, axis=(1, 2)), 'blk')  45.1 us
    reduce_scatter x1, waiting for transfers between devices, on_device_paired(): both = lax.psum_scatter(both, 'blk', scatter_dimension=0, tiled=True)  30.7 us
    unnamed x36, local copies, waits for them, and re-layouts  12.9 us
    ppermute x9, starting transfers between devices, moved(): return lax.ppermute(x, 'blk', route)  12.1 us
  transfers between devices with their start and end apart: 18, of which 12 were waited for; matrix products, arithmetic and copies ran while one was open for 0% of the time, Pallas kernels for 14%

profile of v1, /device:TPU:0, one launch (start us, length us, event | category | flops | bytes accessed | tf_op | source)
XLA Modules:
  0.0 453.0 jit_solution(11048482485372567577)
XLA Ops:
  11.1 1.3 copy.39
  12.5 2.5 fusion.1
  15.0 2.0 copy.40
  18.4 4.7 %collective-permute-done.coef_b = f32[6,128]{1,0:T(8,128)S(1)} collective-permute-done((f32[6,128]{1,0:T(8,128)S(1)}, f32[6,128]{1,0:T(8,128)S(1)}, u32[]{:S(2)}, u32[]{:S(2)}) %collective-permute-start) | collective-permute-done | bytes 3104 | tf_op jit(solution)/shard_map/ppermute | solution.py:311
  23.1 43.7 %all-gather.4.cloned.1.call-done.full = bf16[128,128,128]{2,1,0:T(8,128)(2,1)} async-done(((bf16[16,128,128]{2,1,0:T(8,128)(2,1)}), bf16[128,128,128]{2,1,0:T(8,128)(2,1)}) %all-gather.4.cloned.1.call-update) | async-done | bytes 4194320 | tf_op jit(solution)/shard_map/all_gather | solution.py:327
  66.8 2.2 copy-done.2
  69.0 8.0 %shard_map.104 = s16[2064,128]{1,0:T(8,128)(2,1)} custom-call(s32[1]{0:T(128)} %bitcast.10.place, f32[6,128]{1,0:T(8,128)S(1)} %bitcast.84, f32[6,128]{1,0:T(8,128)S(1)} %collective-permute-done.coef_b, s32[6,128]{1,0:T(8,128)S(1)} %bitcast.97, s32[6,128]{1,0:T(8,128)S(1)} %collective-permute-done.1.from_b, s32[16,8]{1,0:T(8,128)S(1)} %copy.51.inverse, ...), custom_call_target="tpu_custom_call" | custom-call | flops 1610612736 | bytes 8388608 | tf_op jit(solution)/shard_map/pallas_call | solution.py:209
  78.3 7.9 %shard_map.105 = s16[2064,128]{1,0:T(8,128)(2,1)} custom-call(s32[1]{0:T(128)} %bitcast.11.place, f32[6,128]{1,0:T(8,128)S(1)} %bitcast.85, f32[6,128]{1,0:T(8,128)S(1)} %collective-permute-done.coef_b, s32[6,128]{1,0:T(8,128)S(1)} %bitcast.98, s32[6,128]{1,0:T(8,128)S(1)} %collective-permute-done.1.from_b, s32[16,8]{1,0:T(8,128)S(1)} %copy.51.inverse, ...), custom_call_target="tpu_custom_call" | custom-call | flops 1610612736 | bytes 8388608 | tf_op jit(solution)/shard_map/pallas_call | solution.py:209
  86.9 8.0 %shard_map.106 = s16[2064,128]{1,0:T(8,128)(2,1)} custom-call(s32[1]{0:T(128)} %bitcast.12.place, f32[6,128]{1,0:T(8,128)S(1)} %bitcast.86, f32[6,128]{1,0:T(8,128)S(1)} %collective-permute-done.coef_b, s32[6,128]{1,0:T(8,128)S(1)} %bitcast.99, s32[6,128]{1,0:T(8,128)S(1)} %collective-permute-done.1.from_b, s32[16,8]{1,0:T(8,128)S(1)} %copy.51.inverse, ...), custom_call_target="tpu_custom_call" | custom-call | flops 1610612736 | bytes 8388608 | tf_op jit(solution)/shard_map/pallas_call | solution.py:209
  94.9 3.1 collective-permute-start.6
  98.7 1.6 fusion.refs_3_
  100.3 2.2 copy-done.3
  102.5 6.5 %shard_map.103.own = f32[16,128,128]{2,1,0:T(8,128)S(1)} custom-call(s32[1]{0:T(128)} %bitcast.place, f32[6,128]{1,0:T(8,128)S(1)} %bitcast.87, f32[6,128]{1,0:T(8,128)S(1)} %collective-permute-done.coef_b, s32[6,128]{1,0:T(8,128)S(1)} %bitcast.100, s32[6,128]{1,0:T(8,128)S(1)} %collective-permute-done.1.from_b, s32[16,8]{1,0:T(8,128)S(1)} %copy.51.inverse, ...), custom_call_target="tpu_custom_call" | custom-call | flops 1610612736 | bytes 8388608 | tf_op jit(solution)/shard_map/pallas_call | solution.py:209
  109.0 5.8 %collective-permute-done.4.refs_0_ = s16[2064,128]{1,0:T(8,128)(2,1)} collective-permute-done((s16[2064,128]{1,0:T(8,128)(2,1)}, s16[2064,128]{1,0:T(8,128)(2,1)}, u32[]{:S(2)}, u32[]{:S(2)}) %collective-permute-start.4) | collective-permute-done | bytes 528416 | tf_op jit(solution)/shard_map/ppermute | solution.py:308
  114.8 11.2 %collective-permute-done.6.refs_2_ = s16[2064,128]{1,0:T(8,128)(2,1)} collective-permute-done((s16[2064,128]{1,0:T(8,128)(2,1)}, s16[2064,128]{1,0:T(8,128)(2,1)}, u32[]{:S(2)}, u32[]{:S(2)}) %collective-permute-start.6) | collective-permute-done | bytes 528416 | tf_op jit(solution)/shard_map/ppermute | solution.py:308
  126.1 2.1 shard_map.107
  129.3 13.6 %psum.21 = f32[3]{0:T(128)S(1)} all-reduce(f32[3]{0:T(128)S(1)} %reduce_sum.37), channel_id=1, replica_groups=mesh['seg'=4,'blk'=8] {'blk'}, use_global_device_ids=true, to_apply=%region_2.4 | all-reduce | flops 3 | bytes 24 | tf_op jit(solution)/shard_map/psum | solution.py:334
  146.6 2.6 fusion.7
  149.3 45.1 %all-gather.6.cloned.1.call-done.full = bf16[128,128,128]{2,1,0:T(8,128)(2,1)} async-done(((bf16[16,128,128]{2,1,0:T(8,128)(2,1)}), bf16[128,128,128]{2,1,0:T(8,128)(2,1)}) %all-gather.6.cloned.1.call-update) | async-done | bytes 4194320 | tf_op jit(solution)/shard_map/all_gather | solution.py:327
  194.4 2.2 copy-done.5
  196.6 7.2 %shard_map.111 = s16[2064,128]{1,0:T(8,128)(2,1)S(1)} custom-call(s32[1]{0:T(128)} %bitcast.12.place, f32[6,128]{1,0:T(8,128)S(1)} %bitcast.88, f32[6,128]{1,0:T(8,128)S(1)} %collective-permute-done.coef_b, s32[6,128]{1,0:T(8,128)S(1)} %bitcast.101, s32[6,128]{1,0:T(8,128)S(1)} %collective-permute-done.1.from_b, s32[16,8]{1,0:T(8,128)S(1)} %copy.51.inverse, ...), custom_call_target="tpu_custom_call" | custom-call | flops 1610612736 | bytes 8388608 | tf_op jit(solution)/shard_map/pallas_call | solution.py:209
  203.8 1.4 collective-permute-start.9
  205.3 7.2 %shard_map.110 = s16[2064,128]{1,0:T(8,128)(2,1)S(1)} custom-call(s32[1]{0:T(128)} %bitcast.11.place, f32[6,128]{1,0:T(8,128)S(1)} %bitcast.89, f32[6,128]{1,0:T(8,128)S(1)} %collective-permute-done.coef_b, s32[6,128]{1,0:T(8,128)S(1)} %bitcast.102, s32[6,128]{1,0:T(8,128)S(1)} %collective-permute-done.1.from_b, s32[16,8]{1,0:T(8,128)S(1)} %copy.51.inverse, ...), custom_call_target="tpu_custom_call" | custom-call | flops 1610612736 | bytes 8388608 | tf_op jit(solution)/shard_map/pallas_call | solution.py:209
  213.4 7.2 %shard_map.109 = s16[2064,128]{1,0:T(8,128)(2,1)S(1)} custom-call(s32[1]{0:T(128)} %bitcast.10.place, f32[6,128]{1,0:T(8,128)S(1)} %bitcast.90, f32[6,128]{1,0:T(8,128)S(1)} %collective-permute-done.coef_b, s32[6,128]{1,0:T(8,128)S(1)} %bitcast.103, s32[6,128]{1,0:T(8,128)S(1)} %collective-permute-done.1.from_b, s32[16,8]{1,0:T(8,128)S(1)} %copy.51.inverse, ...), custom_call_target="tpu_custom_call" | custom-call | flops 1610612736 | bytes 8388608 | tf_op jit(solution)/shard_map/pallas_call | solution.py:209
  220.6 1.3 collective-permute-start.7
  221.9 6.6 %shard_map.108.own = f32[16,128,128]{2,1,0:T(8,128)S(1)} custom-call(s32[1]{0:T(128)} %bitcast.place, f32[6,128]{1,0:T(8,128)S(1)} %bitcast.91, f32[6,128]{1,0:T(8,128)S(1)} %collective-permute-done.coef_b, s32[6,128]{1,0:T(8,128)S(1)} %bitcast.104, s32[6,128]{1,0:T(8,128)S(1)} %collective-permute-done.1.from_b, s32[16,8]{1,0:T(8,128)S(1)} %copy.51.inverse, ...), custom_call_target="tpu_custom_call" | custom-call | flops 1610612736 | bytes 8388608 | tf_op jit(solution)/shard_map/pallas_call | solution.py:209
  228.5 2.4 collective-permute-done.8.refs_1_
  230.9 21.8 %collective-permute-done.7.refs_0_ = s16[2064,128]{1,0:T(8,128)(2,1)S(1)} collective-permute-done((s16[2064,128]{1,0:T(8,128)(2,1)S(1)}, s16[2064,128]{1,0:T(8,128)(2,1)S(1)}, u32[]{:S(2)}, u32[]{:S(2)}) %collective-permute-start.7) | collective-permute-done | bytes 528416 | tf_op jit(solution)/shard_map/ppermute | solution.py:308
  252.7 1.4 shard_map.112
  255.2 15.7 %psum.22 = f32[3]{0:T(128)S(1)} all-reduce(f32[3]{0:T(128)S(1)} %reduce_sum.38), channel_id=1, replica_groups=mesh['seg'=4,'blk'=8] {'blk'}, use_global_device_ids=true, to_apply=%region_4.6 | all-reduce | flops 3 | bytes 24 | tf_op jit(solution)/shard_map/psum | solution.py:334
  274.6 2.9 fusion.6
  277.6 44.9 %all-gather.8.cloned.1.call-done.full = bf16[128,128,128]{2,1,0:T(8,128)(2,1)} async-done(((bf16[16,128,128]{2,1,0:T(8,128)(2,1)}), bf16[128,128,128]{2,1,0:T(8,128)(2,1)}) %all-gather.8.cloned.1.call-update) | async-done | bytes 4194320 | tf_op jit(solution)/shard_map/all_gather | solution.py:327
  322.5 2.2 copy-done.4
  324.7 7.2 %shard_map.116 = s16[2064,128]{1,0:T(8,128)(2,1)S(1)} custom-call(s32[1]{0:T(128)} %bitcast.12.place, f32[6,128]{1,0:T(8,128)S(1)} %bitcast.92, f32[6,128]{1,0:T(8,128)S(1)} %collective-permute-done.coef_b, s32[6,128]{1,0:T(8,128)S(1)} %bitcast.105, s32[6,128]{1,0:T(8,128)S(1)} %collective-permute-done.1.from_b, s32[16,8]{1,0:T(8,128)S(1)} %copy.51.inverse, ...), custom_call_target="tpu_custom_call" | custom-call | flops 1610612736 | bytes 8388608 | tf_op jit(solution)/shard_map/pallas_call | solution.py:209
  331.9 1.4 collective-permute-start.12
  333.3 7.2 %shard_map.115 = s16[2064,128]{1,0:T(8,128)(2,1)S(1)} custom-call(s32[1]{0:T(128)} %bitcast.11.place, f32[6,128]{1,0:T(8,128)S(1)} %bitcast.93, f32[6,128]{1,0:T(8,128)S(1)} %collective-permute-done.coef_b, s32[6,128]{1,0:T(8,128)S(1)} %bitcast.106, s32[6,128]{1,0:T(8,128)S(1)} %collective-permute-done.1.from_b, s32[16,8]{1,0:T(8,128)S(1)} %copy.51.inverse, ...), custom_call_target="tpu_custom_call" | custom-call | flops 1610612736 | bytes 8388608 | tf_op jit(solution)/shard_map/pallas_call | solution.py:209
  341.2 7.2 %shard_map.114 = s16[2064,128]{1,0:T(8,128)(2,1)S(1)} custom-call(s32[1]{0:T(128)} %bitcast.10.place, f32[6,128]{1,0:T(8,128)S(1)} %bitcast.94, f32[6,128]{1,0:T(8,128)S(1)} %collective-permute-done.coef_b, s32[6,128]{1,0:T(8,128)S(1)} %bitcast.107, s32[6,128]{1,0:T(8,128)S(1)} %collective-permute-done.1.from_b, s32[16,8]{1,0:T(8,128)S(1)} %copy.51.inverse, ...), custom_call_target="tpu_custom_call" | custom-call | flops 1610612736 | bytes 8388608 | tf_op jit(solution)/shard_map/pallas_call | solution.py:209
  348.4 1.3 collective-permute-start.10
  349.7 6.6 %shard_map.113.own = f32[16,128,128]{2,1,0:T(8,128)S(1)} custom-call(s32[1]{0:T(128)} %bitcast.place, f32[6,128]{1,0:T(8,128)S(1)} %bitcast.95, f32[6,128]{1,0:T(8,128)S(1)} %collective-permute-done.coef_b, s32[6,128]{1,0:T(8,128)S(1)} %bitcast.108, s32[6,128]{1,0:T(8,128)S(1)} %collective-permute-done.1.from_b, s32[16,8]{1,0:T(8,128)S(1)} %copy.51.inverse, ...), custom_call_target="tpu_custom_call" | custom-call | flops 1610612736 | bytes 8388608 | tf_op jit(solution)/shard_map/pallas_call | solution.py:209
  356.3 2.6 collective-permute-done.11.refs_1_
  358.9 21.8 %collective-permute-done.10.refs_0_ = s16[2064,128]{1,0:T(8,128)(2,1)S(1)} collective-permute-done((s16[2064,128]{1,0:T(8,128)(2,1)S(1)}, s16[2064,128]{1,0:T(8,128)(2,1)S(1)}, u32[]{:S(2)}, u32[]{:S(2)}) %collective-permute-start.10) | collective-permute-done | bytes 528416 | tf_op jit(solution)/shard_map/ppermute | solution.py:308
  380.7 1.4 shard_map.117
  382.3 15.7 %psum.23 = f32[3]{0:T(128)S(1)} all-reduce(f32[3]{0:T(128)S(1)} %reduce_sum.39), channel_id=1, replica_groups=mesh['seg'=4,'blk'=8] {'blk'}, use_global_device_ids=true, to_apply=%region_6.8 | all-reduce | flops 3 | bytes 24 | tf_op jit(solution)/shard_map/psum | solution.py:334
  401.9 4.0 shard_map.118
  407.0 30.7 %reduce-scatter.2.cloned.1.call-done = f32[256,128]{1,0:T(8,128)} async-done(((f32[2048,128]{1,0:T(8,128)}), f32[256,128]{1,0:T(8,128)}) %reduce-scatter.2.cloned.1.call-update) | async-done | bytes 131088 | tf_op jit(solution)/shard_map/reduce_scatter | solution.py:347
  438.5 3.4 collective-permute-start.13
  441.9 1.9 collective-permute-done.13
  443.8 1.5 fusion.3
  (79 shorter events, 15.1 us)
Async XLA Ops:
  7.2 4.0 copy-start.12
  7.2 59.7 %all-gather.4.cloned.1.call-start = ((), (), s32[]{:S(2)}) async-start(), calls=%async_computation.1 | async-start | bytes 4718592 | tf_op jit(solution)/shard_map/all_gather | solution.py:327
  12.5 4.7 %copy-start = (bf16[1,6,8,128,128]{4,3,2,1,0:T(8,128)(2,1)S(1)}, bf16[1,6,8,128,128]{4,3,2,1,0:T(8,128)(2,1)}, u32[]{:S(2)}) copy-start(bf16[1,6,8,128,128]{4,3,2,1,0:T(8,128)(2,1)} %param.11) | copy-start | bytes 4718596
  12.5 5.2 %copy-start.1 = (bf16[1,6,8,128,128]{4,3,2,1,0:T(8,128)(2,1)S(1)}, bf16[1,6,8,128,128]{4,3,2,1,0:T(8,128)(2,1)}, u32[]{:S(2)}) copy-start(bf16[1,6,8,128,128]{4,3,2,1,0:T(8,128)(2,1)} %param.12) | copy-start | bytes 4718596
  12.5 5.3 %copy-start.14 = (f32[1,6,128]{2,0,1:T(1,128)S(1)}, f32[1,6,128]{2,0,1:T(1,128)}, u32[]{:S(2)}) copy-start(f32[1,6,128]{2,0,1:T(1,128)} %param.13) | copy-start | bytes 9220
  12.5 5.8 %copy-start.15 = (s32[1,6,128]{2,0,1:T(1,128)S(1)}, s32[1,6,128]{2,0,1:T(1,128)}, u32[]{:S(2)}) copy-start(s32[1,6,128]{2,0,1:T(1,128)} %param.14) | copy-start | bytes 9220
  12.5 5.8 %copy-start.13 = (s32[1,16,8]{1,2,0:T(8,128)S(1)}, s32[1,16,8]{1,2,0:T(8,128)}, u32[]{:S(2)}) copy-start(s32[1,16,8]{1,2,0:T(8,128)} %param.15) | copy-start | bytes 1540
  17.1 177.3 %all-gather.6.cloned.1.call-start = ((), (), s32[]{:S(2)}) async-start(), calls=%async_computation.2 | async-start | bytes 4718592 | tf_op jit(solution)/shard_map/all_gather | solution.py:327
  17.1 6.0 %collective-permute-start.2 = (bf16[6,8,128,128]{3,2,1,0:T(8,128)(2,1)S(1)}, bf16[6,8,128,128]{3,2,1,0:T(8,128)(2,1)}, u32[]{:S(2)}, u32[]{:S(2)}) collective-permute-start(bf16[6,8,128,128]{3,2,1,0:T(8,128)(2,1)S(1)} %bitcast.57), channel_id=1, source_target_pairs={{0,1},{1,0},{2,3},{3,2},{4,5},{5,4},{6,7},{7,6},{8,9},{9,8},{10,11... | collective-permute-start | bytes 4718600 | tf_op jit(solution)/shard_map/ppermute | solution.py:311
  17.7 5.4 %collective-permute-start.3 = (bf16[6,8,128,128]{3,2,1,0:T(8,128)(2,1)S(1)}, bf16[6,8,128,128]{3,2,1,0:T(8,128)(2,1)}, u32[]{:S(2)}, u32[]{:S(2)}) collective-permute-start(bf16[6,8,128,128]{3,2,1,0:T(8,128)(2,1)S(1)} %bitcast.70), channel_id=1, source_target_pairs={{0,1},{1,0},{2,3},{3,2},{4,5},{5,4},{6,7},{7,6},{8,9},{9,8},{10,11... | collective-permute-start | bytes 4718600 | tf_op jit(solution)/shard_map/ppermute | solution.py:311
  17.8 5.3 %collective-permute-start = (f32[6,128]{1,0:T(8,128)S(1)}, f32[6,128]{1,0:T(8,128)S(1)}, u32[]{:S(2)}, u32[]{:S(2)}) collective-permute-start(f32[6,128]{1,0:T(8,128)S(1)} %bitcast.83), channel_id=1, source_target_pairs={{0,1},{1,0},{2,3},{3,2},{4,5},{5,4},{6,7},{7,6},{8,9},{9,8},{10,11... | collective-permute-start | bytes 9224 | tf_op jit(solution)/shard_map/ppermute | solution.py:311
  18.2 4.9 %collective-permute-start.1 = (s32[6,128]{1,0:T(8,128)S(1)}, s32[6,128]{1,0:T(8,128)S(1)}, u32[]{:S(2)}, u32[]{:S(2)}) collective-permute-start(s32[6,128]{1,0:T(8,128)S(1)} %bitcast.96), channel_id=1, source_target_pairs={{0,1},{1,0},{2,3},{3,2},{4,5},{5,4},{6,7},{7,6},{8,9},{9,8},{10,11... | collective-permute-start | bytes 9224 | tf_op jit(solution)/shard_map/ppermute | solution.py:311
  66.8 2.2 copy-start.2
  77.0 37.8 %collective-permute-start.4 = (s16[2064,128]{1,0:T(8,128)(2,1)}, s16[2064,128]{1,0:T(8,128)(2,1)}, u32[]{:S(2)}, u32[]{:S(2)}) collective-permute-start(s16[2064,128]{1,0:T(8,128)(2,1)} %shard_map.104), channel_id=1, source_target_pairs={{0,4},{1,5},{2,6},{3,7},{4,0},{5,1},{6,2},{7,3},{8,12},{9,13},{10,... | collective-permute-start | bytes 1585160 | tf_op jit(solution)/shard_map/ppermute | solution.py:308
  86.2 28.6 %collective-permute-start.5 = (s16[2064,128]{1,0:T(8,128)(2,1)}, s16[2064,128]{1,0:T(8,128)(2,1)}, u32[]{:S(2)}, u32[]{:S(2)}) collective-permute-start(s16[2064,128]{1,0:T(8,128)(2,1)} %shard_map.105), channel_id=1, source_target_pairs={{0,2},{1,3},{2,4},{3,5},{4,6},{5,7},{6,0},{7,1},{8,10},{9,11},{10,... | collective-permute-start | bytes 1585160 | tf_op jit(solution)/shard_map/ppermute | solution.py:308
  94.9 31.2 %collective-permute-start.6 = (s16[2064,128]{1,0:T(8,128)(2,1)}, s16[2064,128]{1,0:T(8,128)(2,1)}, u32[]{:S(2)}, u32[]{:S(2)}) collective-permute-start(s16[2064,128]{1,0:T(8,128)(2,1)} %shard_map.106), channel_id=1, source_target_pairs={{0,6},{1,7},{2,0},{3,1},{4,2},{5,3},{6,4},{7,5},{8,14},{9,15},{10,... | collective-permute-start | bytes 1585160 | tf_op jit(solution)/shard_map/ppermute | solution.py:308
  100.3 2.2 copy-start.3
  102.5 23.6 %copy-start.11 = (s32[1,2,8]{2,1,0:T(2,128)S(1)}, s32[1,2,8]{2,1,0:T(2,128)}, u32[]{:S(2)}) copy-start(s32[1,2,8]{2,1,0:T(2,128)} %param.16) | copy-start | bytes 196
  128.2 1.0 copy-start.9
  149.3 173.2 %all-gather.8.cloned.1.call-start = ((), (), s32[]{:S(2)}) async-start(), calls=%async_computation.3 | async-start | bytes 4718592 | tf_op jit(solution)/shard_map/all_gather | solution.py:327
  194.4 2.2 copy-start.5
  203.8 24.6 %collective-permute-start.9 = (s16[2064,128]{1,0:T(8,128)(2,1)S(1)}, s16[2064,128]{1,0:T(8,128)(2,1)S(1)}, u32[]{:S(2)}, u32[]{:S(2)}) collective-permute-start(s16[2064,128]{1,0:T(8,128)(2,1)S(1)} %shard_map.111), channel_id=1, source_target_pairs={{0,6},{1,7},{2,0},{3,1},{4,2},{5,3},{6,4},{7,5},{8,14},{9,15},{10,... | collective-permute-start | bytes 1585160 | tf_op jit(solution)/shard_map/ppermute | solution.py:308
  212.5 18.4 %collective-permute-start.8 = (s16[2064,128]{1,0:T(8,128)(2,1)S(1)}, s16[2064,128]{1,0:T(8,128)(2,1)S(1)}, u32[]{:S(2)}, u32[]{:S(2)}) collective-permute-start(s16[2064,128]{1,0:T(8,128)(2,1)S(1)} %shard_map.110), channel_id=1, source_target_pairs={{0,2},{1,3},{2,4},{3,5},{4,6},{5,7},{6,0},{7,1},{8,10},{9,11},{10,... | collective-permute-start | bytes 1585160 | tf_op jit(solution)/shard_map/ppermute | solution.py:308
  220.6 32.1 %copy-start.6 = (f32[16,128,128]{2,1,0:T(8,128)S(1)}, f32[16,128,128]{2,1,0:T(8,128)}, u32[]{:S(2)}) copy-start(f32[16,128,128]{2,1,0:T(8,128)} %get-tuple-element.25.refs_3_) | copy-start | bytes 3145732
  220.6 32.1 %collective-permute-start.7 = (s16[2064,128]{1,0:T(8,128)(2,1)S(1)}, s16[2064,128]{1,0:T(8,128)(2,1)S(1)}, u32[]{:S(2)}, u32[]{:S(2)}) collective-permute-start(s16[2064,128]{1,0:T(8,128)(2,1)S(1)} %shard_map.109), channel_id=1, source_target_pairs={{0,4},{1,5},{2,6},{3,7},{4,0},{5,1},{6,2},{7,3},{8,12},{9,13},{10,... | collective-permute-start | bytes 1585160 | tf_op jit(solution)/shard_map/ppermute | solution.py:308
  254.1 1.0 copy-start.10
  277.5 160.1 %reduce-scatter.2.cloned.1.call-start = ((), (), s32[]{:S(2)}) async-start(), calls=%async_computation.4 | async-start | bytes 1179648 | tf_op jit(solution)/shard_map/reduce_scatter | solution.py:347
  322.5 2.2 copy-start.4
  331.9 24.4 %collective-permute-start.12 = (s16[2064,128]{1,0:T(8,128)(2,1)S(1)}, s16[2064,128]{1,0:T(8,128)(2,1)S(1)}, u32[]{:S(2)}, u32[]{:S(2)}) collective-permute-start(s16[2064,128]{1,0:T(8,128)(2,1)S(1)} %shard_map.116), channel_id=1, source_target_pairs={{0,6},{1,7},{2,0},{3,1},{4,2},{5,3},{6,4},{7,5},{8,14},{9,15},{10,... | collective-permute-start | bytes 1585160 | tf_op jit(solution)/shard_map/ppermute | solution.py:308
  340.5 18.4 %collective-permute-start.11 = (s16[2064,128]{1,0:T(8,128)(2,1)S(1)}, s16[2064,128]{1,0:T(8,128)(2,1)S(1)}, u32[]{:S(2)}, u32[]{:S(2)}) collective-permute-start(s16[2064,128]{1,0:T(8,128)(2,1)S(1)} %shard_map.115), channel_id=1, source_target_pairs={{0,2},{1,3},{2,4},{3,5},{4,6},{5,7},{6,0},{7,1},{8,10},{9,11},{10,... | collective-permute-start | bytes 1585160 | tf_op jit(solution)/shard_map/ppermute | solution.py:308
  348.4 32.3 %copy-start.7 = (f32[16,128,128]{2,1,0:T(8,128)S(1)}, f32[16,128,128]{2,1,0:T(8,128)}, u32[]{:S(2)}) copy-start(f32[16,128,128]{2,1,0:T(8,128)} %get-tuple-element.23.refs_3_.current) | copy-start | bytes 3145732
  348.4 32.3 %collective-permute-start.10 = (s16[2064,128]{1,0:T(8,128)(2,1)S(1)}, s16[2064,128]{1,0:T(8,128)(2,1)S(1)}, u32[]{:S(2)}, u32[]{:S(2)}) collective-permute-start(s16[2064,128]{1,0:T(8,128)(2,1)S(1)} %shard_map.114), channel_id=1, source_target_pairs={{0,4},{1,5},{2,6},{3,7},{4,0},{5,1},{6,2},{7,3},{8,12},{9,13},{10,... | collective-permute-start | bytes 1585160 | tf_op jit(solution)/shard_map/ppermute | solution.py:308
  380.7 21.2 %copy-start.8 = (f32[16,128,128]{2,1,0:T(8,128)S(1)}, f32[16,128,128]{2,1,0:T(8,128)}, u32[]{:S(2)}) copy-start(f32[16,128,128]{2,1,0:T(8,128)} %get-tuple-element.23.refs_3_.current) | copy-start | bytes 3145732
  438.5 5.3 %collective-permute-start.13 = (f32[128,128]{1,0:T(8,128)S(1)}, f32[128,128]{1,0:T(8,128)S(1)}, u32[]{:S(2)}, u32[]{:S(2)}) collective-permute-start(f32[128,128]{1,0:T(8,128)S(1)} %slice.25), channel_id=1, source_target_pairs={{0,8},{8,16},{16,24},{1,9},{9,17},{17,25},{2,10},{10,18},{18,26},{... | collective-permute-start | bytes 196616 | tf_op jit(solution)/shard_map/ppermute | solution.py:20
Sparse Core Ops, SparseCore 0:
  17.2 49.5 all-gather.3
  149.4 44.9 all-gather.5
  277.7 44.7 all-gather.7
  407.1 30.5 reduce-scatter.1

commit v2 on v0

--- a/solution.py
+++ b/solution.py
@@ -1,6 +1,10 @@
+import functools
+
 import jax
 import jax.numpy as jnp
 from jax import lax
+from jax.experimental import pallas as pl
+from jax.experimental.pallas import tpu as pltpu
 from jax.sharding import PartitionSpec as P
 
 NSEC = 8
@@ -72,7 +76,7 @@
     return (updated, quotient)
 
 
-def on_device(psi_init, env_left, env_right, coef, source, right_sector, sector_sizes, step_size):
+def on_device_general(psi_init, env_left, env_right, coef, source, right_sector, sector_sizes, step_size):
     left_env = env_left[0]
     right_env = env_right[0]
     weights = coef[0]
@@ -119,6 +123,355 @@
     return (current[None], quotient.reshape(1), density[None])
 
 
+BF = jnp.bfloat16
+F32 = jnp.float32
+MIB = 1 << 20
+TOP = 32767.0
+EXP_ROWS = 16
+UNROLL = 2
+ROWS_ROWS = (((1,), (1,)), ((), ()))
+COLS_COLS = (((0,), (0,)), ((), ()))
+SMEM = pl.BlockSpec(memory_space=pltpu.SMEM)
+VMEM = pl.BlockSpec(memory_space=pltpu.VMEM)
+
+
+def parameters(mib):
+    return pltpu.CompilerParams(vmem_limit_bytes=mib * MIB)
+
+
+def terms_kernel(
+    turned, unroll, place, coef_a, coef_b, from_a, from_b, inverse, full,
+    left_a, left_b, right_a, right_b, out_a, out_b, middle,
+):
+    halves = ((coef_a, from_a, left_a, right_a), (coef_b, from_b, left_b, right_b))
+    count = left_a.shape[0]
+    base = place[0] * (2 * NSEC)
+
+    def first(a):
+        for half, (_, sources, left, _) in enumerate(halves):
+            for k in range(count):
+                one = full[sources[k, base + a]]
+                two = full[sources[k, base + NSEC + a]]
+                if turned:
+                    both = jnp.concatenate([one, two], axis=0)
+                    product = lax.dot_general(
+                        left[k, a], both, ROWS_ROWS, preferred_element_type=F32
+                    )
+                else:
+                    both = jnp.concatenate([one, two], axis=1)
+                    product = jnp.dot(left[k, a], both, preferred_element_type=F32)
+                product = product.astype(BF)
+                middle[half * count + k, 0, a] = product[:, :BS]
+                middle[half * count + k, 1, a] = product[:, BS:]
+
+    def second(b):
+        picked = [inverse[place[0] * 2 + t, b] for t in range(2)]
+        sums = [None, None]
+        for half, (weights, _, _, right) in enumerate(halves):
+            for k in range(count):
+                both = jnp.concatenate(
+                    [middle[half * count + k, t, picked[t]] for t in range(2)], axis=0
+                )
+                product = lax.dot_general(right[k, b], both, ROWS_ROWS, preferred_element_type=F32)
+                for t in range(2):
+                    term = product[:, t * BS : (t + 1) * BS] * weights[k, base + t * NSEC + picked[t]]
+                    sums[t] = term if sums[t] is None else sums[t] + term
+        out_a[picked[0]] = sums[0]
+        out_b[picked[1]] = sums[1]
+
+    def run(step):
+        def several(i, carry):
+            for j in range(unroll):
+                step(i * unroll + j)
+            return carry
+
+        lax.fori_loop(0, NSEC // unroll, several, 0)
+
+    run(first)
+    run(second)
+
+
+def terms(turned, place, tables, full, envs):
+    channels = 2 * envs[0].shape[0]
+    half = jax.ShapeDtypeStruct((NSEC, BS, BS), F32)
+    return pl.pallas_call(
+        functools.partial(terms_kernel, turned, UNROLL),
+        out_shape=(half, half),
+        in_specs=[SMEM] * 6 + [VMEM] * 5,
+        out_specs=(VMEM, VMEM),
+        scratch_shapes=[pltpu.VMEM((channels, 2, NSEC, BS, BS), BF)],
+        compiler_params=parameters(24),
+        cost_estimate=pl.CostEstimate(
+            flops=channels * NSEC * 8 * BS**3, bytes_accessed=8 * MIB, transcendentals=0
+        ),
+    )(place, *tables, full, *envs)
+
+
+CODED = jax.ShapeDtypeStruct((NSEC * BS + EXP_ROWS, BS), jnp.int16)
+
+
+def decoded(ref, index):
+    power = ref[NSEC * BS : NSEC * BS + EXP_ROWS, :].astype(jnp.int32).astype(F32)
+    value = ref[index * BS : (index + 1) * BS, :].astype(jnp.int32).astype(F32)
+    return value * jnp.exp2(power[index : index + 1, :])
+
+
+def relay_kernel(*refs):
+    own, out = refs[-2], refs[-1]
+    rows = lax.broadcasted_iota(jnp.int32, (EXP_ROWS, BS), 0)
+    powers = jnp.zeros((EXP_ROWS, BS), jnp.int32)
+    for i in range(NSEC):
+        value = own[i]
+        for ref in refs[:-2]:
+            value = value + decoded(ref, i)
+        most = jnp.max(jnp.max(jnp.abs(value), axis=0, keepdims=True), axis=1, keepdims=True)
+        power = jnp.clip(jnp.ceil(jnp.log2(jnp.maximum(most, 1e-30) / TOP)), -100.0, 100.0)
+        whole = jnp.clip(jnp.round(value * jnp.exp2(-power)), -TOP, TOP)
+        out[i * BS : (i + 1) * BS, :] = whole.astype(jnp.int32).astype(jnp.int16)
+        powers = jnp.where(rows == i, power.astype(jnp.int32), powers)
+    out[NSEC * BS : NSEC * BS + EXP_ROWS, :] = powers.astype(jnp.int16)
+
+
+def relay(arrived, own):
+    return pl.pallas_call(
+        relay_kernel,
+        out_shape=CODED,
+        in_specs=[VMEM] * (len(arrived) + 1),
+        out_specs=VMEM,
+        compiler_params=parameters(8),
+        cost_estimate=pl.CostEstimate(flops=10 * own.size, bytes_accessed=MIB, transcendentals=0),
+    )(*arrived, own)
+
+
+def assemble_kernel(*refs):
+    pieces, out, sems = refs[:-2], refs[-2], refs[-1]
+    size = pieces[0].shape[0]
+    copies = [
+        pltpu.make_async_copy(piece, out.at[pl.ds(n * size, size)], sems.at[n])
+        for n, piece in enumerate(pieces)
+    ]
+    for copy in copies:
+        copy.start()
+    for copy in copies:
+        copy.wait()
+
+
+def assemble(pieces):
+    total = sum(piece.shape[0] for piece in pieces)
+    return pl.pallas_call(
+        assemble_kernel,
+        out_shape=jax.ShapeDtypeStruct((total, BS, BS), BF),
+        in_specs=[pl.BlockSpec(memory_space=pl.ANY)] * len(pieces),
+        out_specs=VMEM,
+        scratch_shapes=[pltpu.SemaphoreType.DMA((len(pieces),))],
+        compiler_params=parameters(8),
+    )(*pieces)
+
+
+def combine_kernel(half, place, sizes, labels, *refs):
+    before, (own, coded, current, applied, sums) = refs[:-5], refs[-5:]
+    down = lax.broadcasted_iota(jnp.int32, (BS, BS), 0)
+    across = lax.broadcasted_iota(jnp.int32, (BS, BS), 1)
+    totals = [jnp.zeros((8, BS), F32) for _ in range(3)]
+    for a in range(NSEC):
+        live = (across < sizes[0, a]) & (down < sizes[1, labels[place[0] * 2 + half, a]])
+        value = jnp.where(live, own[a] + decoded(coded, a), 0.0)
+        applied[a] = value
+        old = current[a]
+        for n, terms_of in enumerate((old * old, old * value, value * value)):
+            totals[n] = totals[n] + jnp.sum(terms_of.reshape(BS // 8, 8, BS), axis=0)
+    rows = lax.broadcasted_iota(jnp.int32, (8, BS), 0)
+    result = jnp.zeros((8, BS), F32)
+    for n in range(3):
+        result = jnp.where(rows == n, jnp.sum(totals[n], axis=0, keepdims=True), result)
+    for ref in before:
+        result = result + ref[...]
+    sums[...] = result
+
+
+def combine(half, place, sizes, labels, before, own, coded, current):
+    return pl.pallas_call(
+        functools.partial(combine_kernel, half),
+        out_shape=(
+            jax.ShapeDtypeStruct(own.shape, F32),
+            jax.ShapeDtypeStruct((8, BS), F32),
+        ),
+        in_specs=[SMEM] * 3 + [VMEM] * (3 + len(before)),
+        out_specs=(VMEM, VMEM),
+        compiler_params=parameters(8),
+        cost_estimate=pl.CostEstimate(flops=10 * own.size, bytes_accessed=2 * MIB, transcendentals=0),
+    )(place, sizes, labels, *before, own, coded, current)
+
+
+def factors(parts, step_len, cells_total):
+    total = (parts[0][...] + parts[2][...]) + (parts[1][...] + parts[3][...])
+    total = jnp.sum(total, axis=1, keepdims=True)
+    square_sum, cross_sum, image_sum = total[0:1], total[1:2], total[2:3]
+    quotient = cross_sum / square_sum
+    new_norm = square_sum + step_len * step_len * (image_sum - quotient * quotient * square_sum)
+    scale = jnp.sqrt(cells_total / new_norm)
+    return (1.0 + step_len * quotient) * scale, step_len * scale, quotient
+
+
+def update_kernel(cells_total, step_len, *refs):
+    parts, (current, applied, out, narrow) = refs[:-4], refs[-4:]
+    keep, take, _ = factors(parts, step_len[0], cells_total)
+    for i in range(current.shape[0]):
+        value = keep * current[i] - take * applied[i]
+        out[i] = value
+        narrow[i] = value.astype(BF)
+
+
+def update(cells_total, step_size, parts, current, applied):
+    return pl.pallas_call(
+        functools.partial(update_kernel, cells_total),
+        out_shape=(
+            jax.ShapeDtypeStruct(current.shape, F32),
+            jax.ShapeDtypeStruct(current.shape, BF),
+        ),
+        in_specs=[SMEM] + [VMEM] * (len(parts) + 2),
+        out_specs=(VMEM, VMEM),
+        compiler_params=parameters(8),
+    )(step_size, *parts, current, applied)
+
+
+def finish_kernel(cells_total, place, step_len, inverse, *refs):
+    parts = refs[:4]
+    current_a, current_b, applied_a, applied_b, psi, energy, keep_rho, give_rho, hold = refs[4:]
+    keep, take, quotient = factors(parts, step_len[0], cells_total)
+    energy[...] = jnp.broadcast_to(quotient, (8, BS))
+    for i in range(NSEC):
+        for t, (current, applied) in enumerate(((current_a, applied_a), (current_b, applied_b))):
+            value = keep * current[i] - take * applied[i]
+            hold[t * NSEC + i] = value
+            psi[t * NSEC + i] = value.T
+
+    def gram(dims, one, two):
+        kw = dict(precision=lax.Precision.HIGHEST, preferred_element_type=F32)
+        return lax.dot_general(one, one, dims, **kw) + lax.dot_general(two, two, dims, **kw)
+
+    core = lax.rem(place[0], 2)
+    for mine, out in ((core, keep_rho), (1 - core, give_rho)):
+        for chip in range(NSEC // 2):
+            sector = 2 * chip + mine
+            out[chip, 0] = gram(COLS_COLS, hold[sector], hold[NSEC + sector])
+            one = hold[inverse[place[0] * 2, sector]]
+            two = hold[NSEC + inverse[place[0] * 2 + 1, sector]]
+            out[chip, 1] = gram(ROWS_ROWS, one, two)
+
+
+def finish(cells_total, place, step_size, inverse, parts, currents, applieds):
+    rho = jax.ShapeDtypeStruct((NSEC // 2, 2, BS, BS), F32)
+    psi = jax.ShapeDtypeStruct((2 * NSEC, BS, BS), F32)
+    return pl.pallas_call(
+        functools.partial(finish_kernel, cells_total),
+        out_shape=(psi, jax.ShapeDtypeStruct((8, BS), F32), rho, rho),
+        in_specs=[SMEM] * 3 + [VMEM] * 8,
+        out_specs=(VMEM,) * 4,
+        scratch_shapes=[pltpu.VMEM(psi.shape, F32)],
+        compiler_params=parameters(24),
+    )(place, step_size, inverse, *parts, *currents, *applieds)
+
+
+def fold_kernel(place, mine, other, *outs):
+    chips = mine.shape[0]
+    for by in range(chips):
+        chip = lax.rem(place[0] // 2 + by, chips)
+        for n in range(2):
+            outs[2 * by + n][...] = mine[chip, n] + other[chip, n]
+
+
+def fold(place, mine, other):
+    chips = mine.shape[0]
+    return pl.pallas_call(
+        fold_kernel,
+        out_shape=(jax.ShapeDtypeStruct((BS, BS), F32),) * (2 * chips),
+        in_specs=[SMEM, VMEM, VMEM],
+        out_specs=(VMEM,) * (2 * chips),
+        compiler_params=parameters(8),
+    )(place, mine, other)
+
+
+def on_device_paired(psi_init, env_left, env_right, coef, source, right_sector, sector_sizes, step_size):
+    count = lax.axis_size("blk")
+    segments = lax.axis_size("seg")
+    line = count // 2
+    me = lax.axis_index("blk")
+    labels = right_sector[0]
+    sizes = sector_sizes[0]
+    cells_total = float(NB * BS * BS)
+
+    def swapped(x):
+        return lax.ppermute(x, "blk", [(i, i ^ 1) for i in range(count)])
+
+    def shifted(x, by=1):
+        return lax.ppermute(x, "blk", [(i, (i + 2 * by) % count) for i in range(count)])
+
+    def handed_on(x, by):
+        route = [
+            (s * count + i, (s + 1) * count + (i + 2 * by) % count)
+            for s in range(segments - 1)
+            for i in range(count)
+        ]
+        return lax.ppermute(x, ("seg", "blk"), route)
+
+    owner = source[0] // (2 * NSEC)
+    plane = (owner % 2) ^ (me % 2)
+    behind = (me // 2 - owner // 2) % line
+    spots = ((plane * line + behind) * (2 * NSEC) + source[0] % (2 * NSEC)).astype(jnp.int32)
+    there = ((((1 - plane) * line + behind)) * (2 * NSEC) + source[0] % (2 * NSEC)).astype(jnp.int32)
+
+    mine = (env_left[0], env_right[0], coef[0])
+    other = tuple(swapped(x) for x in mine)
+    envs = (mine[0], other[0], mine[1], other[1])
+    sector = jnp.arange(NSEC, dtype=jnp.int32)
+    inverse = jnp.sum(
+        jnp.where(labels[:, :, None] == sector[None, None, :], sector[None, :, None], 0), axis=1
+    ).astype(jnp.int32)
+    tables = (mine[2], other[2], spots, swapped(there), inverse)
+    places = [((me - 2 * by) % count).astype(jnp.int32).reshape(1) for by in range(line)]
+
+    own_count = psi_init.shape[1]
+    own_ids = me * own_count + jnp.arange(own_count, dtype=jnp.int32)
+    begin = psi_init[0] * block_mask(own_ids, sizes, labels.reshape(NB))
+    narrow = [begin[t * NSEC : (t + 1) * NSEC].astype(BF) for t in range(2)]
+    current = [jnp.swapaxes(begin[t * NSEC : (t + 1) * NSEC], 1, 2) for t in range(2)]
+    for iteration in range(ITERS):
+        pieces = list(narrow)
+        moving = list(narrow)
+        for _ in range(line - 1):
+            moving = [shifted(x) for x in moving]
+            pieces += moving
+        full = assemble(pieces + [swapped(x) for x in pieces])
+        turned = iteration > 0
+        parts = [terms(turned, places[by], tables, full, envs) for by in (*range(1, line), 0)]
+        moving = [shifted(relay([], parts[0][t])) for t in range(2)]
+        for step in range(1, line - 1):
+            moving = [shifted(relay([moving[t]], parts[step][t])) for t in range(2)]
+        applied, sums = [None, None], []
+        for t in range(2):
+            applied[t], one = combine(
+                t, places[0], sizes, labels, sums, parts[line - 1][t], moving[t], current[t]
+            )
+            sums = [one]
+        chip = sums[0] + swapped(sums[0])
+        sums = [chip] + [shifted(chip, by) for by in range(1, line)]
+        if iteration < ITERS - 1:
+            for t in range(2):
+                current[t], narrow[t] = update(cells_total, step_size, sums, current[t], applied[t])
+    psi, energy, keep_rho, give_rho = finish(
+        cells_total, places[0], step_size, inverse, sums, current, applied
+    )
+    folded = fold(places[0], keep_rho, swapped(give_rho))
+    density = folded[0]
+    for by in range(1, line):
+        density = density + shifted(folded[2 * by], by)
+    for by in range(line):
+        density = density + handed_on(folded[2 * by + 1], by)
+    density = density / float(P_SIZE * BS)
+    return (psi[None], energy[0, :1], density[None])
+
+
 def solution(mesh):
     in_specs = (
         P("seg", "blk", None, None),
@@ -131,6 +484,11 @@
         P("seg"),
     )
     out_specs = (P("seg", "blk", None, None), P("seg"), P("seg", "blk", None))
+    paired = NB // mesh.shape["blk"] == 2 * NSEC and mesh.shape["blk"] == NSEC
     return jax.shard_map(
-        on_device, mesh=mesh, in_specs=in_specs, out_specs=out_specs, check_vma=False
+        on_device_paired if paired else on_device_general,
+        mesh=mesh,
+        in_specs=in_specs,
+        out_specs=out_specs,
+        check_vma=False,
     )

time: 1030 us -> 362 us (0.35)
  waiting for transfers between devices: 456 us -> 165 us
  local copies, waits for them, and re-layouts: 273 us -> 45.9 us
  matrix products: 206 us -> 0 us
  Pallas kernels: 0 us -> 105 us
  blocking collectives: 42.9 us -> 0 us
  starting transfers between devices: 3.86 us -> 41.7 us
  between operations: 26.2 us -> 2.17 us
  other arithmetic: 17.7 us -> 1.25 us
    reduce_scatter x5 -> x0, waiting for transfers between devices: 318 us -> none  [the longest x3 265 us: on_device(): lax.psum_scatter(partial_terms(jnp.int32(0), own_count * lax.axis_size('b...]
    gather x91 -> x0, local copies, waits for them, and re-layouts: 249 us -> none  [the longest x36 116 us: channel(): picked = jnp.take(full_bf, jnp.take(source_one, indices), axis=0)]
    dot_general x22 -> x0, matrix products: 206 us -> none  [the longest x18 199 us: channel(): jnp.einsum('nab,ncb->nac', middle, right_mats, preferred_element_type=jnp...]
    ppermute x1 -> x84, waiting for transfers between devices: 0.01 us -> 165 us  [the longest x48 155 us: shifted(): lax.ppermute(x, 'blk', [(i, (i + 2 * by) % count) for i in range(count)])]
    all_gather x3 -> x0, waiting for transfers between devices: 137 us -> none  [on_device(): lax.all_gather(current.astype(jnp.bfloat16), 'blk', axis=0, tiled=True)]
    pallas_call x0 -> x45, Pallas kernels: none -> 105 us  [the longest x12 78.5 us: terms(): pl.pallas_call(functools.partial(terms_kernel, turned, UNROLL), out_shape...]
    psum x3 -> x0, blocking collectives: 42.9 us -> none  [on_device(): lax.psum((jnp.sum(current * current), jnp.sum(current * applied), jnp.sum...]
    ppermute x1 -> x84, starting transfers between devices: 3.34 us -> 41.7 us  [the longest x48 22.5 us: shifted(): lax.ppermute(x, 'blk', [(i, (i + 2 * by) % count) for i in range(count)])]
  transfers between devices with their start and end apart: 9 -> 84, of which waited for: 8 -> 45; matrix products, arithmetic and copies ran while one was open for 1% -> 6% of each run, Pallas kernels for 0% -> 21%
where the time goes in v2:
time: 362 us; the launch traced here: 360 us
  waiting for transfers between devices  165 us (46%)
  Pallas kernels  105 us (29%)
  local copies, waits for them, and re-layouts  45.9 us (13%)
  starting transfers between devices  41.7 us (12%)
    ppermute x48, waiting for transfers between devices, shifted(): lax.ppermute(x, 'blk', [(i, (i + 2 * by) % count) for i in range(count)])  155 us
    pallas_call x12, Pallas kernels, terms(): pl.pallas_call(functools.partial(terms_kernel, turned, UNROLL), out_shape...  78.5 us
    unnamed x67, local copies, waits for them, and re-layouts  25.4 us
    ppermute x48, starting transfers between devices, shifted(): lax.ppermute(x, 'blk', [(i, (i + 2 * by) % count) for i in range(count)])  22.5 us
    ppermute x4, starting transfers between devices, handed_on(): return lax.ppermute(x, ('seg', 'blk'), route)  14.8 us
    pallas_call x18, Pallas kernels, relay(): pl.pallas_call(relay_kernel, out_shape=CODED, in_specs=[VMEM] * (len(arri...  12.5 us
    ppermute x8, local copies, waits for them, and re-layouts, swapped(): return lax.ppermute(x, 'blk', [(i, i ^ 1) for i in range(count)])  9.7 us
    ppermute x32, waiting for transfers between devices, swapped(): return lax.ppermute(x, 'blk', [(i, i ^ 1) for i in range(count)])  8.44 us
  transfers between devices with their start and end apart: 84, of which 45 were waited for; matrix products, arithmetic and copies ran while one was open for 6% of the time, Pallas kernels for 21%

profile of v2, /device:TPU:0, one launch (start us, length us, event | category | flops | bytes accessed | tf_op | source)
XLA Modules:
  0.0 360.3 jit_solution(8702705132757437236)
XLA Ops:
  7.4 2.6 collective-permute-start.3
  11.8 7.4 %collective-permute-done.3 = bf16[8,128,128]{1,2,0:T(8,128)(2,1)S(1)} collective-permute-done((bf16[8,128,128]{1,2,0:T(8,128)(2,1)S(1)}, bf16[8,128,128]{1,2,0:T(8,128)(2,1)S(1)}, u32[]{:S(2)}, u32[]{:S(2)}) %collective-permute-start.3) | collective-permute-done | bytes 262176 | tf_op jit(solution)/shard_map/ppermute | solution.py:408
  19.2 5.6 %collective-permute-done.2 = bf16[8,128,128]{1,2,0:T(8,128)(2,1)S(1)} collective-permute-done((bf16[8,128,128]{1,2,0:T(8,128)(2,1)S(1)}, bf16[8,128,128]{1,2,0:T(8,128)(2,1)S(1)}, u32[]{:S(2)}, u32[]{:S(2)}) %collective-permute-start.2) | collective-permute-done | bytes 262176 | tf_op jit(solution)/shard_map/ppermute | solution.py:408
  24.9 5.6 %collective-permute-done.5 = bf16[8,128,128]{1,2,0:T(8,128)(2,1)S(1)} collective-permute-done((bf16[8,128,128]{1,2,0:T(8,128)(2,1)S(1)}, bf16[8,128,128]{1,2,0:T(8,128)(2,1)S(1)}, u32[]{:S(2)}, u32[]{:S(2)}) %collective-permute-start.5) | collective-permute-done | bytes 262176 | tf_op jit(solution)/shard_map/ppermute | solution.py:408
  30.5 5.6 %collective-permute-done.4 = bf16[8,128,128]{1,2,0:T(8,128)(2,1)S(1)} collective-permute-done((bf16[8,128,128]{1,2,0:T(8,128)(2,1)S(1)}, bf16[8,128,128]{1,2,0:T(8,128)(2,1)S(1)}, u32[]{:S(2)}, u32[]{:S(2)}) %collective-permute-start.4) | collective-permute-done | bytes 262176 | tf_op jit(solution)/shard_map/ppermute | solution.py:408
  36.1 5.6 %collective-permute-done.7 = bf16[8,128,128]{1,2,0:T(8,128)(2,1)S(1)} collective-permute-done((bf16[8,128,128]{1,2,0:T(8,128)(2,1)S(1)}, bf16[8,128,128]{1,2,0:T(8,128)(2,1)S(1)}, u32[]{:S(2)}, u32[]{:S(2)}) %collective-permute-start.7) | collective-permute-done | bytes 262176 | tf_op jit(solution)/shard_map/ppermute | solution.py:408
  41.7 5.3 %collective-permute-done.6 = bf16[8,128,128]{1,2,0:T(8,128)(2,1)S(1)} collective-permute-done((bf16[8,128,128]{1,2,0:T(8,128)(2,1)S(1)}, bf16[8,128,128]{1,2,0:T(8,128)(2,1)S(1)}, u32[]{:S(2)}, u32[]{:S(2)}) %collective-permute-start.6) | collective-permute-done | bytes 262176 | tf_op jit(solution)/shard_map/ppermute | solution.py:408
  81.0 6.5 %shard_map.105 = (f32[8,128,128]{2,1,0:T(8,128)S(1)}, f32[8,128,128]{2,1,0:T(8,128)S(1)}) custom-call(s32[1]{0:T(128)} %bitcast.9.place, f32[6,128]{1,0:T(8,128)S(1)} %bitcast.94, f32[6,128]{1,0:T(8,128)S(1)} %collective-permute-done.coef_b, s32[6,128]{1,0:T(8,128)S(1)} %get-tuple-element.121.from_a, s32[6,128]{1,0:T(8,128)S(1)} %collective-permute-done.1.from_b, ...), custom_call_target="tpu_custom_call" | custom-call | flops 1610612736 | bytes 8388608 | tf_op jit(solution)/shard_map/pallas_call | solution.py:197
  90.7 2.2 copy-done.3
  92.9 6.5 %shard_map.107 = (f32[8,128,128]{2,1,0:T(8,128)S(1)}, f32[8,128,128]{2,1,0:T(8,128)S(1)}) custom-call(s32[1]{0:T(128)} %bitcast.10.place, f32[6,128]{1,0:T(8,128)S(1)} %bitcast.95, f32[6,128]{1,0:T(8,128)S(1)} %collective-permute-done.coef_b, s32[6,128]{1,0:T(8,128)S(1)} %get-tuple-element.121.from_a, s32[6,128]{1,0:T(8,128)S(1)} %collective-permute-done.1.from_b, ...), custom_call_target="tpu_custom_call" | custom-call | flops 1610612736 | bytes 8388608 | tf_op jit(solution)/shard_map/pallas_call | solution.py:197
  107.0 2.2 copy-done.4
  109.1 6.5 %shard_map.109 = (f32[8,128,128]{2,1,0:T(8,128)S(1)}, f32[8,128,128]{2,1,0:T(8,128)S(1)}) custom-call(s32[1]{0:T(128)} %bitcast.11.place, f32[6,128]{1,0:T(8,128)S(1)} %bitcast.96, f32[6,128]{1,0:T(8,128)S(1)} %collective-permute-done.coef_b, s32[6,128]{1,0:T(8,128)S(1)} %get-tuple-element.121.from_a, s32[6,128]{1,0:T(8,128)S(1)} %collective-permute-done.1.from_b, ...), custom_call_target="tpu_custom_call" | custom-call | flops 1610612736 | bytes 8388608 | tf_op jit(solution)/shard_map/pallas_call | solution.py:197
  122.5 2.2 copy-done.5
  124.7 6.6 %shard_map.104 = (f32[8,128,128]{2,1,0:T(8,128)S(1)}, f32[8,128,128]{2,1,0:T(8,128)S(1)}) custom-call(s32[1]{0:T(128)} %bitcast.place, f32[6,128]{1,0:T(8,128)S(1)} %bitcast.97, f32[6,128]{1,0:T(8,128)S(1)} %collective-permute-done.coef_b, s32[6,128]{1,0:T(8,128)S(1)} %get-tuple-element.121.from_a, s32[6,128]{1,0:T(8,128)S(1)} %collective-permute-done.1.from_b, ...), custom_call_target="tpu_custom_call" | custom-call | flops 1610612736 | bytes 8388608 | tf_op jit(solution)/shard_map/pallas_call | solution.py:197
  140.7 2.6 collective-permute-done.26.refs_2_
  146.5 9.9 %collective-permute-done.29.refs_3_ = bf16[8,128,128]{2,1,0:T(8,128)(2,1)S(1)} collective-permute-done((bf16[8,128,128]{2,1,0:T(8,128)(2,1)S(1)}, bf16[8,128,128]{2,1,0:T(8,128)(2,1)S(1)}, u32[]{:S(2)}, u32[]{:S(2)}) %collective-permute-start.29) | collective-permute-done | bytes 262176 | tf_op jit(solution)/shard_map/ppermute | solution.py:408
  156.4 5.6 %collective-permute-done.28.refs_2_ = bf16[8,128,128]{2,1,0:T(8,128)(2,1)S(1)} collective-permute-done((bf16[8,128,128]{2,1,0:T(8,128)(2,1)S(1)}, bf16[8,128,128]{2,1,0:T(8,128)(2,1)S(1)}, u32[]{:S(2)}, u32[]{:S(2)}) %collective-permute-start.28) | collective-permute-done | bytes 262176 | tf_op jit(solution)/shard_map/ppermute | solution.py:408
  162.5 5.1 %collective-permute-done.31.refs_5_ = bf16[8,128,128]{2,1,0:T(8,128)(2,1)S(1)} collective-permute-done((bf16[8,128,128]{2,1,0:T(8,128)(2,1)S(1)}, bf16[8,128,128]{2,1,0:T(8,128)(2,1)S(1)}, u32[]{:S(2)}, u32[]{:S(2)}) %collective-permute-start.31) | collective-permute-done | bytes 262176 | tf_op jit(solution)/shard_map/ppermute | solution.py:408
  167.6 5.6 %collective-permute-done.30.refs_4_ = bf16[8,128,128]{2,1,0:T(8,128)(2,1)S(1)} collective-permute-done((bf16[8,128,128]{2,1,0:T(8,128)(2,1)S(1)}, bf16[8,128,128]{2,1,0:T(8,128)(2,1)S(1)}, u32[]{:S(2)}, u32[]{:S(2)}) %collective-permute-start.30) | collective-permute-done | bytes 262176 | tf_op jit(solution)/shard_map/ppermute | solution.py:408
  173.9 5.0 %collective-permute-done.33.refs_7_ = bf16[8,128,128]{2,1,0:T(8,128)(2,1)S(1)} collective-permute-done((bf16[8,128,128]{2,1,0:T(8,128)(2,1)S(1)}, bf16[8,128,128]{2,1,0:T(8,128)(2,1)S(1)}, u32[]{:S(2)}, u32[]{:S(2)}) %collective-permute-start.33) | collective-permute-done | bytes 262176 | tf_op jit(solution)/shard_map/ppermute | solution.py:408
  178.9 3.1 collective-permute-done.32.refs_6_
  184.0 6.6 %shard_map.120 = (f32[8,128,128]{2,1,0:T(8,128)S(1)}, f32[8,128,128]{2,1,0:T(8,128)S(1)}) custom-call(s32[1]{0:T(128)} %bitcast.9.place, f32[6,128]{1,0:T(8,128)S(1)} %bitcast.98, f32[6,128]{1,0:T(8,128)S(1)} %collective-permute-done.coef_b, s32[6,128]{1,0:T(8,128)S(1)} %get-tuple-element.121.from_a, s32[6,128]{1,0:T(8,128)S(1)} %collective-permute-done.1.from_b, ...), custom_call_target="tpu_custom_call" | custom-call | flops 1610612736 | bytes 8388608 | tf_op jit(solution)/shard_map/pallas_call | solution.py:197
  191.1 6.6 %shard_map.122 = (f32[8,128,128]{2,1,0:T(8,128)S(1)}, f32[8,128,128]{2,1,0:T(8,128)S(1)}) custom-call(s32[1]{0:T(128)} %bitcast.10.place, f32[6,128]{1,0:T(8,128)S(1)} %bitcast.99, f32[6,128]{1,0:T(8,128)S(1)} %collective-permute-done.coef_b, s32[6,128]{1,0:T(8,128)S(1)} %get-tuple-element.121.from_a, s32[6,128]{1,0:T(8,128)S(1)} %collective-permute-done.1.from_b, ...), custom_call_target="tpu_custom_call" | custom-call | flops 1610612736 | bytes 8388608 | tf_op jit(solution)/shard_map/pallas_call | solution.py:197
  197.6 4.2 %collective-permute-done.42.refs_0_ = s16[1040,128]{1,0:T(8,128)(2,1)S(1)} collective-permute-done((s16[1040,128]{1,0:T(8,128)(2,1)S(1)}, s16[1040,128]{1,0:T(8,128)(2,1)S(1)}, u32[]{:S(2)}, u32[]{:S(2)}) %collective-permute-start.42) | collective-permute-done | bytes 266272 | tf_op jit(solution)/shard_map/ppermute | solution.py:408
  202.2 5.4 %collective-permute-done.45.refs_0_ = s16[1040,128]{1,0:T(8,128)(2,1)S(1)} collective-permute-done((s16[1040,128]{1,0:T(8,128)(2,1)S(1)}, s16[1040,128]{1,0:T(8,128)(2,1)S(1)}, u32[]{:S(2)}, u32[]{:S(2)}) %collective-permute-start.45) | collective-permute-done | bytes 266272 | tf_op jit(solution)/shard_map/ppermute | solution.py:408
  207.9 6.6 %shard_map.124 = (f32[8,128,128]{2,1,0:T(8,128)S(1)}, f32[8,128,128]{2,1,0:T(8,128)S(1)}) custom-call(s32[1]{0:T(128)} %bitcast.11.place, f32[6,128]{1,0:T(8,128)S(1)} %bitcast.100, f32[6,128]{1,0:T(8,128)S(1)} %collective-permute-done.coef_b, s32[6,128]{1,0:T(8,128)S(1)} %get-tuple-element.121.from_a, s32[6,128]{1,0:T(8,128)S(1)} %collective-permute-done.1.from_b, ...), custom_call_target="tpu_custom_call" | custom-call | flops 1610612736 | bytes 8388608 | tf_op jit(solution)/shard_map/pallas_call | solution.py:197
  214.8 3.9 %collective-permute-done.46.refs_0_ = s16[1040,128]{1,0:T(8,128)(2,1)S(1)} collective-permute-done((s16[1040,128]{1,0:T(8,128)(2,1)S(1)}, s16[1040,128]{1,0:T(8,128)(2,1)S(1)}, u32[]{:S(2)}, u32[]{:S(2)}) %collective-permute-start.46) | collective-permute-done | bytes 266272 | tf_op jit(solution)/shard_map/ppermute | solution.py:408
  219.0 6.6 %shard_map.119 = (f32[8,128,128]{2,1,0:T(8,128)S(1)}, f32[8,128,128]{2,1,0:T(8,128)S(1)}) custom-call(s32[1]{0:T(128)} %bitcast.place, f32[6,128]{1,0:T(8,128)S(1)} %bitcast.101, f32[6,128]{1,0:T(8,128)S(1)} %collective-permute-done.coef_b, s32[6,128]{1,0:T(8,128)S(1)} %get-tuple-element.121.from_a, s32[6,128]{1,0:T(8,128)S(1)} %collective-permute-done.1.from_b, ...), custom_call_target="tpu_custom_call" | custom-call | flops 1610612736 | bytes 8388608 | tf_op jit(solution)/shard_map/pallas_call | solution.py:197
  226.5 3.0 collective-permute-done.47.refs_2_
  240.6 9.0 %collective-permute-done.53.refs_3_ = bf16[8,128,128]{2,1,0:T(8,128)(2,1)S(1)} collective-permute-done((bf16[8,128,128]{2,1,0:T(8,128)(2,1)S(1)}, bf16[8,128,128]{2,1,0:T(8,128)(2,1)S(1)}, u32[]{:S(2)}, u32[]{:S(2)}) %collective-permute-start.53) | collective-permute-done | bytes 262176 | tf_op jit(solution)/shard_map/ppermute | solution.py:408
  249.6 5.6 %collective-permute-done.52.refs_2_ = bf16[8,128,128]{2,1,0:T(8,128)(2,1)S(1)} collective-permute-done((bf16[8,128,128]{2,1,0:T(8,128)(2,1)S(1)}, bf16[8,128,128]{2,1,0:T(8,128)(2,1)S(1)}, u32[]{:S(2)}, u32[]{:S(2)}) %collective-permute-start.52) | collective-permute-done | bytes 262176 | tf_op jit(solution)/shard_map/ppermute | solution.py:408
  255.7 5.1 %collective-permute-done.55.refs_5_ = bf16[8,128,128]{2,1,0:T(8,128)(2,1)S(1)} collective-permute-done((bf16[8,128,128]{2,1,0:T(8,128)(2,1)S(1)}, bf16[8,128,128]{2,1,0:T(8,128)(2,1)S(1)}, u32[]{:S(2)}, u32[]{:S(2)}) %collective-permute-start.55) | collective-permute-done | bytes 262176 | tf_op jit(solution)/shard_map/ppermute | solution.py:408
  260.8 5.6 %collective-permute-done.54.refs_4_ = bf16[8,128,128]{2,1,0:T(8,128)(2,1)S(1)} collective-permute-done((bf16[8,128,128]{2,1,0:T(8,128)(2,1)S(1)}, bf16[8,128,128]{2,1,0:T(8,128)(2,1)S(1)}, u32[]{:S(2)}, u32[]{:S(2)}) %collective-permute-start.54) | collective-permute-done | bytes 262176 | tf_op jit(solution)/shard_map/ppermute | solution.py:408
  267.1 5.0 %collective-permute-done.57.refs_7_ = bf16[8,128,128]{2,1,0:T(8,128)(2,1)S(1)} collective-permute-done((bf16[8,128,128]{2,1,0:T(8,128)(2,1)S(1)}, bf16[8,128,128]{2,1,0:T(8,128)(2,1)S(1)}, u32[]{:S(2)}, u32[]{:S(2)}) %collective-permute-start.57) | collective-permute-done | bytes 262176 | tf_op jit(solution)/shard_map/ppermute | solution.py:408
  272.1 3.4 collective-permute-done.56.refs_6_
  277.5 6.6 %shard_map.135 = (f32[8,128,128]{2,1,0:T(8,128)S(1)}, f32[8,128,128]{2,1,0:T(8,128)S(1)}) custom-call(s32[1]{0:T(128)} %bitcast.9.place, f32[6,128]{1,0:T(8,128)S(1)} %bitcast.102, f32[6,128]{1,0:T(8,128)S(1)} %collective-permute-done.coef_b, s32[6,128]{1,0:T(8,128)S(1)} %get-tuple-element.121.from_a, s32[6,128]{1,0:T(8,128)S(1)} %collective-permute-done.1.from_b, ...), custom_call_target="tpu_custom_call" | custom-call | flops 1610612736 | bytes 8388608 | tf_op jit(solution)/shard_map/pallas_call | solution.py:197
  284.6 6.6 %shard_map.137 = (f32[8,128,128]{2,1,0:T(8,128)S(1)}, f32[8,128,128]{2,1,0:T(8,128)S(1)}) custom-call(s32[1]{0:T(128)} %bitcast.10.place, f32[6,128]{1,0:T(8,128)S(1)} %bitcast.103, f32[6,128]{1,0:T(8,128)S(1)} %collective-permute-done.coef_b, s32[6,128]{1,0:T(8,128)S(1)} %get-tuple-element.121.from_a, s32[6,128]{1,0:T(8,128)S(1)} %collective-permute-done.1.from_b, ...), custom_call_target="tpu_custom_call" | custom-call | flops 1610612736 | bytes 8388608 | tf_op jit(solution)/shard_map/pallas_call | solution.py:197
  291.1 4.2 %collective-permute-done.66.refs_0_ = s16[1040,128]{1,0:T(8,128)(2,1)S(1)} collective-permute-done((s16[1040,128]{1,0:T(8,128)(2,1)S(1)}, s16[1040,128]{1,0:T(8,128)(2,1)S(1)}, u32[]{:S(2)}, u32[]{:S(2)}) %collective-permute-start.66) | collective-permute-done | bytes 266272 | tf_op jit(solution)/shard_map/ppermute | solution.py:408
  295.7 5.4 %collective-permute-done.69.refs_0_ = s16[1040,128]{1,0:T(8,128)(2,1)S(1)} collective-permute-done((s16[1040,128]{1,0:T(8,128)(2,1)S(1)}, s16[1040,128]{1,0:T(8,128)(2,1)S(1)}, u32[]{:S(2)}, u32[]{:S(2)}) %collective-permute-start.69) | collective-permute-done | bytes 266272 | tf_op jit(solution)/shard_map/ppermute | solution.py:408
  301.4 6.6 %shard_map.139 = (f32[8,128,128]{2,1,0:T(8,128)S(1)}, f32[8,128,128]{2,1,0:T(8,128)S(1)}) custom-call(s32[1]{0:T(128)} %bitcast.11.place, f32[6,128]{1,0:T(8,128)S(1)} %bitcast.104, f32[6,128]{1,0:T(8,128)S(1)} %collective-permute-done.coef_b, s32[6,128]{1,0:T(8,128)S(1)} %get-tuple-element.121.from_a, s32[6,128]{1,0:T(8,128)S(1)} %collective-permute-done.1.from_b, ...), custom_call_target="tpu_custom_call" | custom-call | flops 1610612736 | bytes 8388608 | tf_op jit(solution)/shard_map/pallas_call | solution.py:197
  308.3 3.8 %collective-permute-done.70.refs_0_ = s16[1040,128]{1,0:T(8,128)(2,1)S(1)} collective-permute-done((s16[1040,128]{1,0:T(8,128)(2,1)S(1)}, s16[1040,128]{1,0:T(8,128)(2,1)S(1)}, u32[]{:S(2)}, u32[]{:S(2)}) %collective-permute-start.70) | collective-permute-done | bytes 266272 | tf_op jit(solution)/shard_map/ppermute | solution.py:408
  312.5 6.6 %shard_map.134 = (f32[8,128,128]{2,1,0:T(8,128)S(1)}, f32[8,128,128]{2,1,0:T(8,128)S(1)}) custom-call(s32[1]{0:T(128)} %bitcast.place, f32[6,128]{1,0:T(8,128)S(1)} %bitcast.105, f32[6,128]{1,0:T(8,128)S(1)} %collective-permute-done.coef_b, s32[6,128]{1,0:T(8,128)S(1)} %get-tuple-element.121.from_a, s32[6,128]{1,0:T(8,128)S(1)} %collective-permute-done.1.from_b, ...), custom_call_target="tpu_custom_call" | custom-call | flops 1610612736 | bytes 8388608 | tf_op jit(solution)/shard_map/pallas_call | solution.py:197
  320.0 3.0 collective-permute-done.71.refs_2_
  331.8 5.0 %shard_map.146 = (f32[16,128,128]{2,1,0:T(8,128)}, f32[8,128]{1,0:T(8,128)S(1)}, f32[4,2,128,128]{3,2,1,0:T(8,128)S(1)}, f32[4,2,128,128]{3,2,1,0:T(8,128)S(1)}) custom-call(s32[1]{0:T(128)} %bitcast.place, f32[1]{0:T(128)S(6)} %copy.141.step_len, s32[16,8]{1,0:T(8,128)S(1)} %copy.97.inverse, f32[8,128]{1,0:T(8,128)S(1)} %add.144.refs_0_, ...), custom_call_target="tpu_custom_call" | custom-call | tf_op jit(solution)/shard_map/pallas_call | solution.py:366
  342.9 3.4 collective-permute-start.80
  346.3 3.2 collective-permute-start.81
  349.5 3.5 collective-permute-start.82
  353.0 4.8 %collective-permute-start.83 = (f32[128,128]{1,0:T(8,128)S(1)}, f32[128,128]{1,0:T(8,128)S(1)}, u32[]{:S(2)}, u32[]{:S(2)}) collective-permute-start(f32[128,128]{1,0:T(8,128)S(1)} %get-tuple-element.115), channel_id=1, source_target_pairs={{0,14},{1,15},{2,8},{3,9},{4,10},{5,11},{6,12},{7,13},{8,22},{9,23... | collective-permute-start | bytes 196616 | tf_op jit(solution)/shard_map/ppermute | solution.py:416
  (274 shorter events, 111.8 us)
Async XLA Ops:
  0.6 77.9 %collective-permute-start.16 = (bf16[6,8,128,128]{3,2,1,0:T(8,128)(2,1)}, bf16[6,8,128,128]{3,2,1,0:T(8,128)(2,1)}, u32[]{:S(2)}, u32[]{:S(2)}) collective-permute-start(bf16[6,8,128,128]{3,2,1,0:T(8,128)(2,1)} %bitcast.67), channel_id=1, source_target_pairs={{0,1},{1,0},{2,3},{3,2},{4,5},{5,4},{6,7},{7,6},{8,9},{9,8},{10,11... | collective-permute-start | bytes 4718600 | tf_op jit(solution)/shard_map/ppermute | solution.py:405
  1.2 77.3 %collective-permute-start.17 = (bf16[6,8,128,128]{3,2,1,0:T(8,128)(2,1)}, bf16[6,8,128,128]{3,2,1,0:T(8,128)(2,1)}, u32[]{:S(2)}, u32[]{:S(2)}) collective-permute-start(bf16[6,8,128,128]{3,2,1,0:T(8,128)(2,1)} %bitcast.80), channel_id=1, source_target_pairs={{0,1},{1,0},{2,3},{3,2},{4,5},{5,4},{6,7},{7,6},{8,9},{9,8},{10,11... | collective-permute-start | bytes 4718600 | tf_op jit(solution)/shard_map/ppermute | solution.py:405
  7.4 11.8 %collective-permute-start.3 = (bf16[8,128,128]{1,2,0:T(8,128)(2,1)S(1)}, bf16[8,128,128]{1,2,0:T(8,128)(2,1)S(1)}, u32[]{:S(2)}, u32[]{:S(2)}) collective-permute-start(bf16[8,128,128]{1,2,0:T(8,128)(2,1)S(1)} %get-tuple-element.118), channel_id=1, source_target_pairs={{0,2},{1,3},{2,4},{3,5},{4,6},{5,7},{6,0},{7,1},{8,10},{9,11},{10,... | collective-permute-start | bytes 786440 | tf_op jit(solution)/shard_map/ppermute | solution.py:408
  10.2 14.6 %collective-permute-start.2 = (bf16[8,128,128]{1,2,0:T(8,128)(2,1)S(1)}, bf16[8,128,128]{1,2,0:T(8,128)(2,1)S(1)}, u32[]{:S(2)}, u32[]{:S(2)}) collective-permute-start(bf16[8,128,128]{1,2,0:T(8,128)(2,1)S(1)} %get-tuple-element.119), channel_id=1, source_target_pairs={{0,2},{1,3},{2,4},{3,5},{4,6},{5,7},{6,0},{7,1},{8,10},{9,11},{10,... | collective-permute-start | bytes 786440 | tf_op jit(solution)/shard_map/ppermute | solution.py:408
  19.2 11.2 %collective-permute-start.5 = (bf16[8,128,128]{1,2,0:T(8,128)(2,1)S(1)}, bf16[8,128,128]{1,2,0:T(8,128)(2,1)S(1)}, u32[]{:S(2)}, u32[]{:S(2)}) collective-permute-start(bf16[8,128,128]{1,2,0:T(8,128)(2,1)S(1)} %collective-permute-done.3), channel_id=1, source_target_pairs={{0,2},{1,3},{2,4},{3,5},{4,6},{5,7},{6,0},{7,1},{8,10},{9,11},{10,... | collective-permute-start | bytes 786440 | tf_op jit(solution)/shard_map/ppermute | solution.py:408
  24.8 11.2 %collective-permute-start.4 = (bf16[8,128,128]{1,2,0:T(8,128)(2,1)S(1)}, bf16[8,128,128]{1,2,0:T(8,128)(2,1)S(1)}, u32[]{:S(2)}, u32[]{:S(2)}) collective-permute-start(bf16[8,128,128]{1,2,0:T(8,128)(2,1)S(1)} %collective-permute-done.2), channel_id=1, source_target_pairs={{0,2},{1,3},{2,4},{3,5},{4,6},{5,7},{6,0},{7,1},{8,10},{9,11},{10,... | collective-permute-start | bytes 786440 | tf_op jit(solution)/shard_map/ppermute | solution.py:408
  30.5 11.2 %collective-permute-start.7 = (bf16[8,128,128]{1,2,0:T(8,128)(2,1)S(1)}, bf16[8,128,128]{1,2,0:T(8,128)(2,1)S(1)}, u32[]{:S(2)}, u32[]{:S(2)}) collective-permute-start(bf16[8,128,128]{1,2,0:T(8,128)(2,1)S(1)} %collective-permute-done.5), channel_id=1, source_target_pairs={{0,2},{1,3},{2,4},{3,5},{4,6},{5,7},{6,0},{7,1},{8,10},{9,11},{10,... | collective-permute-start | bytes 786440 | tf_op jit(solution)/shard_map/ppermute | solution.py:408
  36.1 11.0 %collective-permute-start.6 = (bf16[8,128,128]{1,2,0:T(8,128)(2,1)S(1)}, bf16[8,128,128]{1,2,0:T(8,128)(2,1)S(1)}, u32[]{:S(2)}, u32[]{:S(2)}) collective-permute-start(bf16[8,128,128]{1,2,0:T(8,128)(2,1)S(1)} %collective-permute-done.4), channel_id=1, source_target_pairs={{0,2},{1,3},{2,4},{3,5},{4,6},{5,7},{6,0},{7,1},{8,10},{9,11},{10,... | collective-permute-start | bytes 786440 | tf_op jit(solution)/shard_map/ppermute | solution.py:408
  36.1 11.0 %collective-permute-start.12 = (bf16[8,128,128]{1,2,0:T(8,128)(2,1)S(1)}, bf16[8,128,128]{1,2,0:T(8,128)(2,1)}, u32[]{:S(2)}, u32[]{:S(2)}) collective-permute-start(bf16[8,128,128]{1,2,0:T(8,128)(2,1)S(1)} %collective-permute-done.4), channel_id=1, source_target_pairs={{0,1},{1,0},{2,3},{3,2},{4,5},{5,4},{6,7},{7,6},{8,9},{9,8},{10,11... | collective-permute-start | bytes 786440 | tf_op jit(solution)/shard_map/ppermute | solution.py:405
  47.1 14.9 %collective-permute-start.14 = (bf16[8,128,128]{1,2,0:T(8,128)(2,1)S(1)}, bf16[8,128,128]{1,2,0:T(8,128)(2,1)}, u32[]{:S(2)}, u32[]{:S(2)}) collective-permute-start(bf16[8,128,128]{1,2,0:T(8,128)(2,1)S(1)} %collective-permute-done.6), channel_id=1, source_target_pairs={{0,1},{1,0},{2,3},{3,2},{4,5},{5,4},{6,7},{7,6},{8,9},{9,8},{10,11... | collective-permute-start | bytes 786440 | tf_op jit(solution)/shard_map/ppermute | solution.py:405
  47.1 31.4 %collective-permute-start.1 = (s32[6,128]{1,0:T(8,128)S(1)}, s32[6,128]{1,0:T(8,128)S(1)}, u32[]{:S(2)}, u32[]{:S(2)}) collective-permute-start(s32[6,128]{1,0:T(8,128)S(1)} %get-tuple-element.120), channel_id=1, source_target_pairs={{0,1},{1,0},{2,3},{3,2},{4,5},{5,4},{6,7},{7,6},{8,9},{9,8},{10,11... | collective-permute-start | bytes 9224 | tf_op jit(solution)/shard_map/ppermute | solution.py:405
  47.7 30.9 %collective-permute-start = (f32[6,128]{1,0:T(8,128)S(1)}, f32[6,128]{1,0:T(8,128)S(1)}, u32[]{:S(2)}, u32[]{:S(2)}) collective-permute-start(f32[6,128]{1,0:T(8,128)S(1)} %bitcast.93), channel_id=1, source_target_pairs={{0,1},{1,0},{2,3},{3,2},{4,5},{5,4},{6,7},{7,6},{8,9},{9,8},{10,11... | collective-permute-start | bytes 9224 | tf_op jit(solution)/shard_map/ppermute | solution.py:405
  88.5 11.4 %collective-permute-start.21 = (s16[1040,128]{1,0:T(8,128)(2,1)}, s16[1040,128]{1,0:T(8,128)(2,1)}, u32[]{:S(2)}, u32[]{:S(2)}) collective-permute-start(s16[1040,128]{1,0:T(8,128)(2,1)} %shard_map.112), channel_id=1, source_target_pairs={{0,2},{1,3},{2,4},{3,5},{4,6},{5,7},{6,0},{7,1},{8,10},{9,11},{10,... | collective-permute-start | bytes 798728 | tf_op jit(solution)/shard_map/ppermute | solution.py:408
  89.4 15.6 %collective-permute-start.18 = (s16[1040,128]{1,0:T(8,128)(2,1)}, s16[1040,128]{1,0:T(8,128)(2,1)}, u32[]{:S(2)}, u32[]{:S(2)}) collective-permute-start(s16[1040,128]{1,0:T(8,128)(2,1)} %shard_map.106), channel_id=1, source_target_pairs={{0,2},{1,3},{2,4},{3,5},{4,6},{5,7},{6,0},{7,1},{8,10},{9,11},{10,... | collective-permute-start | bytes 798728 | tf_op jit(solution)/shard_map/ppermute | solution.py:408
  101.8 13.9 %collective-permute-start.22 = (s16[1040,128]{1,0:T(8,128)(2,1)}, s16[1040,128]{1,0:T(8,128)(2,1)}, u32[]{:S(2)}, u32[]{:S(2)}) collective-permute-start(s16[1040,128]{1,0:T(8,128)(2,1)} %shard_map.113), channel_id=1, source_target_pairs={{0,2},{1,3},{2,4},{3,5},{4,6},{5,7},{6,0},{7,1},{8,10},{9,11},{10,... | collective-permute-start | bytes 798728 | tf_op jit(solution)/shard_map/ppermute | solution.py:408
  107.0 10.7 %collective-permute-start.19 = (s16[1040,128]{1,0:T(8,128)(2,1)}, s16[1040,128]{1,0:T(8,128)(2,1)}, u32[]{:S(2)}, u32[]{:S(2)}) collective-permute-start(s16[1040,128]{1,0:T(8,128)(2,1)} %shard_map.108), channel_id=1, source_target_pairs={{0,2},{1,3},{2,4},{3,5},{4,6},{5,7},{6,0},{7,1},{8,10},{9,11},{10,... | collective-permute-start | bytes 798728 | tf_op jit(solution)/shard_map/ppermute | solution.py:408
  117.7 16.9 %collective-permute-start.23 = (s16[1040,128]{1,0:T(8,128)(2,1)}, s16[1040,128]{1,0:T(8,128)(2,1)}, u32[]{:S(2)}, u32[]{:S(2)}) collective-permute-start(s16[1040,128]{1,0:T(8,128)(2,1)} %shard_map.114), channel_id=1, source_target_pairs={{0,2},{1,3},{2,4},{3,5},{4,6},{5,7},{6,0},{7,1},{8,10},{9,11},{10,... | collective-permute-start | bytes 798728 | tf_op jit(solution)/shard_map/ppermute | solution.py:408
  119.6 13.7 %collective-permute-start.20 = (s16[1040,128]{1,0:T(8,128)(2,1)}, s16[1040,128]{1,0:T(8,128)(2,1)}, u32[]{:S(2)}, u32[]{:S(2)}) collective-permute-start(s16[1040,128]{1,0:T(8,128)(2,1)} %shard_map.110), channel_id=1, source_target_pairs={{0,2},{1,3},{2,4},{3,5},{4,6},{5,7},{6,0},{7,1},{8,10},{9,11},{10,... | collective-permute-start | bytes 798728 | tf_op jit(solution)/shard_map/ppermute | solution.py:408
  145.4 11.0 %collective-permute-start.29 = (bf16[8,128,128]{2,1,0:T(8,128)(2,1)S(1)}, bf16[8,128,128]{2,1,0:T(8,128)(2,1)S(1)}, u32[]{:S(2)}, u32[]{:S(2)}) collective-permute-start(bf16[8,128,128]{2,1,0:T(8,128)(2,1)S(1)} %get-tuple-element.73.refs_1_), channel_id=1, source_target_pairs={{0,2},{1,3},{2,4},{3,5},{4,6},{5,7},{6,0},{7,1},{8,10},{9,11},{10,... | collective-permute-start | bytes 786440 | tf_op jit(solution)/shard_map/ppermute | solution.py:408
  145.7 16.3 %collective-permute-start.28 = (bf16[8,128,128]{2,1,0:T(8,128)(2,1)S(1)}, bf16[8,128,128]{2,1,0:T(8,128)(2,1)S(1)}, u32[]{:S(2)}, u32[]{:S(2)}) collective-permute-start(bf16[8,128,128]{2,1,0:T(8,128)(2,1)S(1)} %get-tuple-element.71.refs_0_), channel_id=1, source_target_pairs={{0,2},{1,3},{2,4},{3,5},{4,6},{5,7},{6,0},{7,1},{8,10},{9,11},{10,... | collective-permute-start | bytes 786440 | tf_op jit(solution)/shard_map/ppermute | solution.py:408
  156.4 11.2 %collective-permute-start.31 = (bf16[8,128,128]{2,1,0:T(8,128)(2,1)S(1)}, bf16[8,128,128]{2,1,0:T(8,128)(2,1)S(1)}, u32[]{:S(2)}, u32[]{:S(2)}) collective-permute-start(bf16[8,128,128]{2,1,0:T(8,128)(2,1)S(1)} %collective-permute-done.29.refs_3_), channel_id=1, source_target_pairs={{0,2},{1,3},{2,4},{3,5},{4,6},{5,7},{6,0},{7,1},{8,10},{9,11},{10,... | collective-permute-start | bytes 786440 | tf_op jit(solution)/shard_map/ppermute | solution.py:408
  162.0 11.2 %collective-permute-start.30 = (bf16[8,128,128]{2,1,0:T(8,128)(2,1)S(1)}, bf16[8,128,128]{2,1,0:T(8,128)(2,1)S(1)}, u32[]{:S(2)}, u32[]{:S(2)}) collective-permute-start(bf16[8,128,128]{2,1,0:T(8,128)(2,1)S(1)} %collective-permute-done.28.refs_2_), channel_id=1, source_target_pairs={{0,2},{1,3},{2,4},{3,5},{4,6},{5,7},{6,0},{7,1},{8,10},{9,11},{10,... | collective-permute-start | bytes 786440 | tf_op jit(solution)/shard_map/ppermute | solution.py:408
  162.0 11.2 %collective-permute-start.35 = (bf16[8,128,128]{2,1,0:T(8,128)(2,1)S(1)}, bf16[8,128,128]{2,1,0:T(8,128)(2,1)S(1)}, u32[]{:S(2)}, u32[]{:S(2)}) collective-permute-start(bf16[8,128,128]{2,1,0:T(8,128)(2,1)S(1)} %get-tuple-element.73.refs_1_), channel_id=1, source_target_pairs={{0,1},{1,0},{2,3},{3,2},{4,5},{5,4},{6,7},{7,6},{8,9},{9,8},{10,11... | collective-permute-start | bytes 786440 | tf_op jit(solution)/shard_map/ppermute | solution.py:405
  162.0 11.2 %collective-permute-start.34 = (bf16[8,128,128]{2,1,0:T(8,128)(2,1)S(1)}, bf16[8,128,128]{2,1,0:T(8,128)(2,1)S(1)}, u32[]{:S(2)}, u32[]{:S(2)}) collective-permute-start(bf16[8,128,128]{2,1,0:T(8,128)(2,1)S(1)} %get-tuple-element.71.refs_0_), channel_id=1, source_target_pairs={{0,1},{1,0},{2,3},{3,2},{4,5},{5,4},{6,7},{7,6},{8,9},{9,8},{10,11... | collective-permute-start | bytes 786440 | tf_op jit(solution)/shard_map/ppermute | solution.py:405
  162.5 11.2 %collective-permute-start.37 = (bf16[8,128,128]{2,1,0:T(8,128)(2,1)S(1)}, bf16[8,128,128]{2,1,0:T(8,128)(2,1)S(1)}, u32[]{:S(2)}, u32[]{:S(2)}) collective-permute-start(bf16[8,128,128]{2,1,0:T(8,128)(2,1)S(1)} %collective-permute-done.29.refs_3_), channel_id=1, source_target_pairs={{0,1},{1,0},{2,3},{3,2},{4,5},{5,4},{6,7},{7,6},{8,9},{9,8},{10,11... | collective-permute-start | bytes 786440 | tf_op jit(solution)/shard_map/ppermute | solution.py:405
  167.6 11.2 %collective-permute-start.33 = (bf16[8,128,128]{2,1,0:T(8,128)(2,1)S(1)}, bf16[8,128,128]{2,1,0:T(8,128)(2,1)S(1)}, u32[]{:S(2)}, u32[]{:S(2)}) collective-permute-start(bf16[8,128,128]{2,1,0:T(8,128)(2,1)S(1)} %collective-permute-done.31.refs_5_), channel_id=1, source_target_pairs={{0,2},{1,3},{2,4},{3,5},{4,6},{5,7},{6,0},{7,1},{8,10},{9,11},{10,... | collective-permute-start | bytes 786440 | tf_op jit(solution)/shard_map/ppermute | solution.py:408
  190.7 11.1 %collective-permute-start.42 = (s16[1040,128]{1,0:T(8,128)(2,1)S(1)}, s16[1040,128]{1,0:T(8,128)(2,1)S(1)}, u32[]{:S(2)}, u32[]{:S(2)}) collective-permute-start(s16[1040,128]{1,0:T(8,128)(2,1)S(1)} %shard_map.121), channel_id=1, source_target_pairs={{0,2},{1,3},{2,4},{3,5},{4,6},{5,7},{6,0},{7,1},{8,10},{9,11},{10,... | collective-permute-start | bytes 798728 | tf_op jit(solution)/shard_map/ppermute | solution.py:408
  191.0 16.6 %collective-permute-start.45 = (s16[1040,128]{1,0:T(8,128)(2,1)S(1)}, s16[1040,128]{1,0:T(8,128)(2,1)S(1)}, u32[]{:S(2)}, u32[]{:S(2)}) collective-permute-start(s16[1040,128]{1,0:T(8,128)(2,1)S(1)} %shard_map.127), channel_id=1, source_target_pairs={{0,2},{1,3},{2,4},{3,5},{4,6},{5,7},{6,0},{7,1},{8,10},{9,11},{10,... | collective-permute-start | bytes 798728 | tf_op jit(solution)/shard_map/ppermute | solution.py:408
  202.1 12.3 %collective-permute-start.43 = (s16[1040,128]{1,0:T(8,128)(2,1)S(1)}, s16[1040,128]{1,0:T(8,128)(2,1)S(1)}, u32[]{:S(2)}, u32[]{:S(2)}) collective-permute-start(s16[1040,128]{1,0:T(8,128)(2,1)S(1)} %shard_map.123), channel_id=1, source_target_pairs={{0,2},{1,3},{2,4},{3,5},{4,6},{5,7},{6,0},{7,1},{8,10},{9,11},{10,... | collective-permute-start | bytes 798728 | tf_op jit(solution)/shard_map/ppermute | solution.py:408
  207.8 10.8 %collective-permute-start.46 = (s16[1040,128]{1,0:T(8,128)(2,1)S(1)}, s16[1040,128]{1,0:T(8,128)(2,1)S(1)}, u32[]{:S(2)}, u32[]{:S(2)}) collective-permute-start(s16[1040,128]{1,0:T(8,128)(2,1)S(1)} %shard_map.128), channel_id=1, source_target_pairs={{0,2},{1,3},{2,4},{3,5},{4,6},{5,7},{6,0},{7,1},{8,10},{9,11},{10,... | collective-permute-start | bytes 798728 | tf_op jit(solution)/shard_map/ppermute | solution.py:408
  214.7 10.8 %collective-permute-start.44 = (s16[1040,128]{1,0:T(8,128)(2,1)S(1)}, s16[1040,128]{1,0:T(8,128)(2,1)S(1)}, u32[]{:S(2)}, u32[]{:S(2)}) collective-permute-start(s16[1040,128]{1,0:T(8,128)(2,1)S(1)} %shard_map.125), channel_id=1, source_target_pairs={{0,2},{1,3},{2,4},{3,5},{4,6},{5,7},{6,0},{7,1},{8,10},{9,11},{10,... | collective-permute-start | bytes 798728 | tf_op jit(solution)/shard_map/ppermute | solution.py:408
  238.6 11.0 %collective-permute-start.53 = (bf16[8,128,128]{2,1,0:T(8,128)(2,1)S(1)}, bf16[8,128,128]{2,1,0:T(8,128)(2,1)S(1)}, u32[]{:S(2)}, u32[]{:S(2)}) collective-permute-start(bf16[8,128,128]{2,1,0:T(8,128)(2,1)S(1)} %get-tuple-element.89.refs_1_), channel_id=1, source_target_pairs={{0,2},{1,3},{2,4},{3,5},{4,6},{5,7},{6,0},{7,1},{8,10},{9,11},{10,... | collective-permute-start | bytes 786440 | tf_op jit(solution)/shard_map/ppermute | solution.py:408
  238.9 16.3 %collective-permute-start.52 = (bf16[8,128,128]{2,1,0:T(8,128)(2,1)S(1)}, bf16[8,128,128]{2,1,0:T(8,128)(2,1)S(1)}, u32[]{:S(2)}, u32[]{:S(2)}) collective-permute-start(bf16[8,128,128]{2,1,0:T(8,128)(2,1)S(1)} %get-tuple-element.87.refs_0_), channel_id=1, source_target_pairs={{0,2},{1,3},{2,4},{3,5},{4,6},{5,7},{6,0},{7,1},{8,10},{9,11},{10,... | collective-permute-start | bytes 786440 | tf_op jit(solution)/shard_map/ppermute | solution.py:408
  249.6 11.2 %collective-permute-start.55 = (bf16[8,128,128]{2,1,0:T(8,128)(2,1)S(1)}, bf16[8,128,128]{2,1,0:T(8,128)(2,1)S(1)}, u32[]{:S(2)}, u32[]{:S(2)}) collective-permute-start(bf16[8,128,128]{2,1,0:T(8,128)(2,1)S(1)} %collective-permute-done.53.refs_3_), channel_id=1, source_target_pairs={{0,2},{1,3},{2,4},{3,5},{4,6},{5,7},{6,0},{7,1},{8,10},{9,11},{10,... | collective-permute-start | bytes 786440 | tf_op jit(solution)/shard_map/ppermute | solution.py:408
  255.2 11.2 %collective-permute-start.54 = (bf16[8,128,128]{2,1,0:T(8,128)(2,1)S(1)}, bf16[8,128,128]{2,1,0:T(8,128)(2,1)S(1)}, u32[]{:S(2)}, u32[]{:S(2)}) collective-permute-start(bf16[8,128,128]{2,1,0:T(8,128)(2,1)S(1)} %collective-permute-done.52.refs_2_), channel_id=1, source_target_pairs={{0,2},{1,3},{2,4},{3,5},{4,6},{5,7},{6,0},{7,1},{8,10},{9,11},{10,... | collective-permute-start | bytes 786440 | tf_op jit(solution)/shard_map/ppermute | solution.py:408
  255.2 11.2 %collective-permute-start.59 = (bf16[8,128,128]{2,1,0:T(8,128)(2,1)S(1)}, bf16[8,128,128]{2,1,0:T(8,128)(2,1)S(1)}, u32[]{:S(2)}, u32[]{:S(2)}) collective-permute-start(bf16[8,128,128]{2,1,0:T(8,128)(2,1)S(1)} %get-tuple-element.89.refs_1_), channel_id=1, source_target_pairs={{0,1},{1,0},{2,3},{3,2},{4,5},{5,4},{6,7},{7,6},{8,9},{9,8},{10,11... | collective-permute-start | bytes 786440 | tf_op jit(solution)/shard_map/ppermute | solution.py:405
  255.2 11.2 %collective-permute-start.58 = (bf16[8,128,128]{2,1,0:T(8,128)(2,1)S(1)}, bf16[8,128,128]{2,1,0:T(8,128)(2,1)S(1)}, u32[]{:S(2)}, u32[]{:S(2)}) collective-permute-start(bf16[8,128,128]{2,1,0:T(8,128)(2,1)S(1)} %get-tuple-element.87.refs_0_), channel_id=1, source_target_pairs={{0,1},{1,0},{2,3},{3,2},{4,5},{5,4},{6,7},{7,6},{8,9},{9,8},{10,11... | collective-permute-start | bytes 786440 | tf_op jit(solution)/shard_map/ppermute | solution.py:405
  255.7 11.2 %collective-permute-start.61 = (bf16[8,128,128]{2,1,0:T(8,128)(2,1)S(1)}, bf16[8,128,128]{2,1,0:T(8,128)(2,1)S(1)}, u32[]{:S(2)}, u32[]{:S(2)}) collective-permute-start(bf16[8,128,128]{2,1,0:T(8,128)(2,1)S(1)} %collective-permute-done.53.refs_3_), channel_id=1, source_target_pairs={{0,1},{1,0},{2,3},{3,2},{4,5},{5,4},{6,7},{7,6},{8,9},{9,8},{10,11... | collective-permute-start | bytes 786440 | tf_op jit(solution)/shard_map/ppermute | solution.py:405
  260.8 11.2 %collective-permute-start.57 = (bf16[8,128,128]{2,1,0:T(8,128)(2,1)S(1)}, bf16[8,128,128]{2,1,0:T(8,128)(2,1)S(1)}, u32[]{:S(2)}, u32[]{:S(2)}) collective-permute-start(bf16[8,128,128]{2,1,0:T(8,128)(2,1)S(1)} %collective-permute-done.55.refs_5_), channel_id=1, source_target_pairs={{0,2},{1,3},{2,4},{3,5},{4,6},{5,7},{6,0},{7,1},{8,10},{9,11},{10,... | collective-permute-start | bytes 786440 | tf_op jit(solution)/shard_map/ppermute | solution.py:408
  284.2 11.1 %collective-permute-start.66 = (s16[1040,128]{1,0:T(8,128)(2,1)S(1)}, s16[1040,128]{1,0:T(8,128)(2,1)S(1)}, u32[]{:S(2)}, u32[]{:S(2)}) collective-permute-start(s16[1040,128]{1,0:T(8,128)(2,1)S(1)} %shard_map.136), channel_id=1, source_target_pairs={{0,2},{1,3},{2,4},{3,5},{4,6},{5,7},{6,0},{7,1},{8,10},{9,11},{10,... | collective-permute-start | bytes 798728 | tf_op jit(solution)/shard_map/ppermute | solution.py:408
  284.5 16.6 %collective-permute-start.69 = (s16[1040,128]{1,0:T(8,128)(2,1)S(1)}, s16[1040,128]{1,0:T(8,128)(2,1)S(1)}, u32[]{:S(2)}, u32[]{:S(2)}) collective-permute-start(s16[1040,128]{1,0:T(8,128)(2,1)S(1)} %shard_map.142), channel_id=1, source_target_pairs={{0,2},{1,3},{2,4},{3,5},{4,6},{5,7},{6,0},{7,1},{8,10},{9,11},{10,... | collective-permute-start | bytes 798728 | tf_op jit(solution)/shard_map/ppermute | solution.py:408
  295.6 12.3 %collective-permute-start.67 = (s16[1040,128]{1,0:T(8,128)(2,1)S(1)}, s16[1040,128]{1,0:T(8,128)(2,1)S(1)}, u32[]{:S(2)}, u32[]{:S(2)}) collective-permute-start(s16[1040,128]{1,0:T(8,128)(2,1)S(1)} %shard_map.138), channel_id=1, source_target_pairs={{0,2},{1,3},{2,4},{3,5},{4,6},{5,7},{6,0},{7,1},{8,10},{9,11},{10,... | collective-permute-start | bytes 798728 | tf_op jit(solution)/shard_map/ppermute | solution.py:408
  301.3 10.8 %collective-permute-start.70 = (s16[1040,128]{1,0:T(8,128)(2,1)S(1)}, s16[1040,128]{1,0:T(8,128)(2,1)S(1)}, u32[]{:S(2)}, u32[]{:S(2)}) collective-permute-start(s16[1040,128]{1,0:T(8,128)(2,1)S(1)} %shard_map.143), channel_id=1, source_target_pairs={{0,2},{1,3},{2,4},{3,5},{4,6},{5,7},{6,0},{7,1},{8,10},{9,11},{10,... | collective-permute-start | bytes 798728 | tf_op jit(solution)/shard_map/ppermute | solution.py:408
  308.2 10.8 %collective-permute-start.68 = (s16[1040,128]{1,0:T(8,128)(2,1)S(1)}, s16[1040,128]{1,0:T(8,128)(2,1)S(1)}, u32[]{:S(2)}, u32[]{:S(2)}) collective-permute-start(s16[1040,128]{1,0:T(8,128)(2,1)S(1)} %shard_map.140), channel_id=1, source_target_pairs={{0,2},{1,3},{2,4},{3,5},{4,6},{5,7},{6,0},{7,1},{8,10},{9,11},{10,... | collective-permute-start | bytes 798728 | tf_op jit(solution)/shard_map/ppermute | solution.py:408
  338.9 14.1 %collective-permute-start.78 = (f32[128,128]{1,0:T(8,128)S(1)}, f32[128,128]{1,0:T(8,128)S(1)}, u32[]{:S(2)}, u32[]{:S(2)}) collective-permute-start(f32[128,128]{1,0:T(8,128)S(1)} %get-tuple-element.110), channel_id=1, source_target_pairs={{0,4},{1,5},{2,6},{3,7},{4,0},{5,1},{6,2},{7,3},{8,12},{9,13},{10,... | collective-permute-start | bytes 196616 | tf_op jit(solution)/shard_map/ppermute | solution.py:408
  340.8 17.5 %collective-permute-start.79 = (f32[128,128]{1,0:T(8,128)S(1)}, f32[128,128]{1,0:T(8,128)S(1)}, u32[]{:S(2)}, u32[]{:S(2)}) collective-permute-start(f32[128,128]{1,0:T(8,128)S(1)} %get-tuple-element.111), channel_id=1, source_target_pairs={{0,6},{1,7},{2,0},{3,1},{4,2},{5,3},{6,4},{7,5},{8,14},{9,15},{10,... | collective-permute-start | bytes 196616 | tf_op jit(solution)/shard_map/ppermute | solution.py:408
  342.9 15.4 %collective-permute-start.80 = (f32[128,128]{1,0:T(8,128)S(1)}, f32[128,128]{1,0:T(8,128)S(1)}, u32[]{:S(2)}, u32[]{:S(2)}) collective-permute-start(f32[128,128]{1,0:T(8,128)S(1)} %get-tuple-element.112), channel_id=1, source_target_pairs={{0,8},{1,9},{2,10},{3,11},{4,12},{5,13},{6,14},{7,15},{8,16},{9,17... | collective-permute-start | bytes 196616 | tf_op jit(solution)/shard_map/ppermute | solution.py:416
  346.3 12.0 %collective-permute-start.81 = (f32[128,128]{1,0:T(8,128)S(1)}, f32[128,128]{1,0:T(8,128)S(1)}, u32[]{:S(2)}, u32[]{:S(2)}) collective-permute-start(f32[128,128]{1,0:T(8,128)S(1)} %get-tuple-element.113), channel_id=1, source_target_pairs={{0,10},{1,11},{2,12},{3,13},{4,14},{5,15},{6,8},{7,9},{8,18},{9,19... | collective-permute-start | bytes 196616 | tf_op jit(solution)/shard_map/ppermute | solution.py:416
  (68 other events, 405.9 us)
